TPU v7x, 128 devices: a whole 4x4x4 slice. The times are simulated.
128 devices in a mesh: req: 4 (over y), seq: 32 (over x, z, core).
Axes of the slice: x: 4, y: 4, z: 4, core: 2. Of those that a mesh axis runs over, the one named last changes fastest.
Arguments:
- hidden_in: bfloat16 [4, 4096, 1600], P('req', 'seq'), may hold values from -6 to 6
- mamba_in: bfloat16 [4, 4096, 3200], P('req', 'seq'), may hold values from -6 to 6
- conv_weight: float32 [4, 3200], replicated, may hold values from -3 to 3
- conv_bias: float32 [3200], replicated, may hold values from -3 to 3
- x_proj: bfloat16 [3200, 132], replicated, may hold values from -0.109375 to 0.109375
- dt_proj: bfloat16 [100, 3200], replicated, may hold values from -0.625 to 0.625
- dt_bias: float32 [3200], replicated, may hold values from -2 to 0.5
- decay_rate: float32 [3200], replicated, may hold values from 2.4414063e-05 to 0.05
- skip_gain: float32 [3200], replicated, may hold values from 0.5 to 1.5
- out_proj: bfloat16 [3200, 1600], replicated, may hold values from -0.109375 to 0.109375
- norm_gain: float32 [1600], replicated, may hold values from 0.3 to 1.7
- mlp_gate: bfloat16 [1600, 5504], P(None, 'req'), may hold values from -0.15625 to 0.15625
- mlp_up: bfloat16 [1600, 5504], P(None, 'req'), may hold values from -0.15625 to 0.15625
- mlp_down: bfloat16 [5504, 1600], P('req'), may hold values from -0.078125 to 0.078125
- cache_state: float32 [4, 32, 16, 3200], P('req', 'seq'), may hold values from -6 to 6
- cache_edge: bfloat16 [4, 32, 3, 3200], P('req', 'seq'), may hold values from -6 to 6
- req_lengths: int32 [4, 4], P('req'), may hold values from 1 to 3072, 4096 in all within a row
- cont_flag: int32 [4, 4], P('req'), may hold values from 0 to 1, as said below
- cache_source: int32 [4, 4], P('req'), may hold values from 0 to 31, as said below
- owner_slot: int32 [4, 4], P('req'), may hold values from 0 to 31, as said below
Outputs:
- block_out: bfloat16 [4, 4096, 1600], P('req', 'seq')
- new_state: float32 [4, 32, 16, 3200], P('req', 'seq')
- new_edge: bfloat16 [4, 32, 3, 3200], P('req', 'seq')
Inputs may be any that keep to these rules, and one draw needn't show every extreme that they name: `req_lengths`: each row sums to 4096; its largest entry is exactly 3072. `owner_slot`: the 4 entries of a row are distinct; slots 0 and 31 each own a request of every group. `cont_flag`: request 0 of every group continues; request 1 of group 0 does not; the others continue with probability one half. `cache_source`: request 0 reads slot 16 in groups 0, 4, 8 ..., slot 31 in groups 1, 5 ..., slot 0 in groups 2, 6 ..., slot 1 in groups 3, 7 ...; other requests read any slot.
All inputs are finite; a program needn't handle non-finite values.
Results may differ from a plain program's by a relative error of at most 0.007.
Values may be sent and summed in bfloat16 or wider, within the bound.
A program may use at most 256 MiB of HBM per device.

v0:
```python
import functools

import jax
import jax.numpy as jnp
from jax import lax
from jax.experimental import pallas as pl
from jax.experimental.pallas import tpu as pltpu
from jax.sharding import PartitionSpec as P

STATE = 16
EDGE = 3
NORM_EPS = 1e-06
LANES = 128
FAR = 1e30
HIGHEST_PREC = lax.Precision.HIGHEST
VMEM = pltpu.VMEM
SMEM = pltpu.SMEM


def vspec():
    return pl.BlockSpec(memory_space=VMEM)


def sspec():
    return pl.BlockSpec(memory_space=SMEM)


def col_block(width):
    return 640 if width % 640 == 0 else LANES


def segment(info, r, rows):
    begin = jnp.int32(0)
    for q in range(r):
        begin = begin + info[q]
    end = begin + info[r]
    first = info[16]
    low = jnp.clip(begin - first, 0, rows)
    high = jnp.clip(end - first, 0, rows)
    fresh = begin >= first
    ends = (end > first) & (end <= first + rows)
    return begin, low, high, fresh, ends


def token_stage(
    info,
    x_ref,
    halo_ref,
    edge_ref,
    start_ref,
    conv_w_ref,
    conv_b_ref,
    x_proj_ref,
    dt_proj_ref,
    dt_bias_ref,
    decay_ref,
    mixed_ref,
    step_ref,
    proj_ref,
    end_ref,
    sum_ref,
    last_edge_ref,
    ext,
    mixed_b,
    suffix,
    b_wide,
):
    rows, inner = x_ref.shape
    width = col_block(inner)
    rank = dt_proj_ref.shape[0]
    ext[pl.ds(0, 16), :] = halo_ref[...].astype(jnp.float32)
    ext[pl.ds(16, rows), :] = x_ref[...].astype(jnp.float32)
    requests = start_ref.shape[0]
    first_pos = info[16]
    position = first_pos + lax.broadcasted_iota(jnp.int32, (rows, LANES), 0)
    marks = [segment(info, r, rows) for r in range(requests)]
    begin = jnp.zeros((rows, LANES), jnp.int32)
    request = jnp.zeros((rows, LANES), jnp.int32)
    last_begin, last_req = jnp.int32(0), jnp.int32(0)
    for r in range(1, requests):
        reached = position >= marks[r][0]
        begin = jnp.where(reached, marks[r][0], begin)
        request = jnp.where(reached, r, request)
        inside = first_pos + rows - 1 >= marks[r][0]
        last_begin = jnp.where(inside, marks[r][0], last_begin)
        last_req = jnp.where(inside, r, last_req)
    offset = position - begin
    in_last = (position >= last_begin).astype(jnp.float32)
    edge_id = lax.broadcasted_iota(jnp.int32, (rows, 16), 1)
    hots = []
    for lag in (1, 2, 3):
        want = request * EDGE + EDGE + offset - lag
        hit = (edge_id == want[:, :16]) & (offset[:, :16] < lag)
        hots.append(hit.astype(jnp.float32).astype(jnp.bfloat16))

    keep = {}
    for lag in (1, 2, 3):
        keep[lag] = jnp.concatenate([offset] * (width // LANES), axis=1) >= lag
    for first in range(0, inner, width):
        cols = pl.ds(first, width)
        edges = edge_ref[:, cols]
        total = conv_b_ref[:, cols] + conv_w_ref[pl.ds(3, 1), cols] * ext[pl.ds(16, rows), cols]
        for lag in (1, 2, 3):
            near = ext[pl.ds(16 - lag, rows), cols]
            far = jnp.dot(hots[lag - 1], edges, preferred_element_type=jnp.float32)
            row = jnp.where(keep[lag], near, far)
            total = total + conv_w_ref[pl.ds(3 - lag, 1), cols] * row
        mixed = (total / (1.0 + jnp.exp(-total))).astype(jnp.bfloat16)
        mixed_b[:, cols] = mixed
        mixed_ref[:, cols] = mixed.astype(jnp.float32)

    proj = jnp.dot(mixed_b[...], x_proj_ref[...], preferred_element_type=jnp.float32)
    proj_ref[...] = proj
    for s in range(STATE):
        b_wide[s] = jnp.broadcast_to(proj[:, rank + s : rank + s + 1], (rows, LANES))
    dt_low = proj[:, :rank].astype(jnp.bfloat16)
    row_id = lax.broadcasted_iota(jnp.int32, (rows, rows), 0)
    col_id = lax.broadcasted_iota(jnp.int32, (rows, rows), 1)
    later = (col_id > row_id).astype(jnp.bfloat16)
    for first in range(0, inner, width):
        cols = pl.ds(first, width)
        v = jnp.dot(dt_low, dt_proj_ref[:, cols], preferred_element_type=jnp.float32)
        v = v + dt_bias_ref[:, cols]
        step = jnp.maximum(v, 0.0) + jnp.log1p(jnp.exp(-jnp.abs(v)))
        step_ref[:, cols] = step
        high = step.astype(jnp.bfloat16)
        rest = step - high.astype(jnp.float32)
        mid = rest.astype(jnp.bfloat16)
        low = (rest - mid.astype(jnp.float32)).astype(jnp.bfloat16)
        after = (
            jnp.dot(later, high, preferred_element_type=jnp.float32)
            + jnp.dot(later, mid, preferred_element_type=jnp.float32)
            + jnp.dot(later, low, preferred_element_type=jnp.float32)
        )
        suffix[:, cols] = after

    starts_here = (last_begin >= first_pos).astype(jnp.int32)
    flag = jnp.full((1, LANES), starts_here, jnp.int32).astype(jnp.float32)
    power = (lax.broadcasted_iota(jnp.int32, (STATE, LANES), 0) + 1).astype(jnp.float32)

    def one_tile(j, carry):
        cols = pl.ds(pl.multiple_of(j * LANES, LANES), LANES)
        rate = decay_ref[:, cols]
        acc = [jnp.zeros((8, LANES), jnp.float32) for _ in range(STATE)]
        since = jnp.zeros((8, LANES), jnp.float32)
        for tile in range(rows // 8):
            here = pl.ds(tile * 8, 8)
            fade = jnp.exp(-rate * suffix[here, cols])
            step = step_ref[here, cols] * in_last[tile * 8 : tile * 8 + 8]
            since = since + step
            push = step * mixed_ref[here, cols]
            for s in range(STATE):
                push = push * fade
                acc[s] = acc[s] + push * b_wide[s, here, :]
        ends = jnp.concatenate([jnp.sum(a, axis=0, keepdims=True) for a in acc], axis=0)
        since = jnp.sum(since, axis=0, keepdims=True)
        seed = jnp.exp(-(rate * since) * power) * start_ref[last_req, :, cols].astype(jnp.float32)
        end_ref[:, cols] = ends + flag * seed
        sum_ref[:, cols] = jnp.where(flag > 0.5, FAR, since)
        return carry

    lax.fori_loop(0, inner // LANES, one_tile, 0)
    row_of = lax.broadcasted_iota(jnp.int32, (16, LANES), 0)
    from_of = lax.broadcasted_iota(jnp.int32, (16, LANES), 1)
    near_at = jnp.full((16, LANES), -1, jnp.int32)
    far_at = jnp.full((16, LANES), -1, jnp.int32)
    for r in range(requests):
        _, _, high, _, ends = marks[r]
        size = info[r]
        for j in range(EDGE):
            lag = EDGE - 1 - j
            near = jnp.where(ends & (size > lag), high + 15 - lag, -1)
            far = jnp.where(ends & (size <= lag), r * EDGE + EDGE + size - 1 - lag, -1)
            near_at = jnp.where(row_of == r * EDGE + j, near, near_at)
            far_at = jnp.where(row_of == r * EDGE + j, far, far_at)

    def hot_rows(at, count):
        return (from_of[:, :count] == at[:, :count]).astype(jnp.float32).astype(jnp.bfloat16)

    for first in range(0, inner, width):
        cols = pl.ds(first, width)
        last_edge_ref[:, cols] = (
            jnp.dot(hot_rows(near_at - 16, rows), x_ref[:, cols], preferred_element_type=jnp.float32)
            + jnp.dot(hot_rows(near_at, 16), halo_ref[:, cols], preferred_element_type=jnp.float32)
            + jnp.dot(hot_rows(far_at, 16), edge_ref[:, cols], preferred_element_type=jnp.float32)
        )


def token_call(info, args, rows, inner, proj_width):
    f32 = jnp.float32
    return pl.pallas_call(
        token_stage,
        out_shape=(
            jax.ShapeDtypeStruct((rows, inner), f32),
            jax.ShapeDtypeStruct((rows, inner), f32),
            jax.ShapeDtypeStruct((rows, proj_width), f32),
            jax.ShapeDtypeStruct((STATE, inner), f32),
            jax.ShapeDtypeStruct((1, inner), f32),
            jax.ShapeDtypeStruct((16, inner), f32),
        ),
        in_specs=[sspec()] + [vspec()] * len(args),
        out_specs=tuple([vspec()] * 6),
        scratch_shapes=[
            VMEM((rows + 16, inner), f32),
            VMEM((rows, inner), jnp.bfloat16),
            VMEM((rows, inner), f32),
            VMEM((STATE, rows, LANES), f32),
        ],
        compiler_params=pltpu.CompilerParams(vmem_limit_bytes=40 << 20),
        cost_estimate=pl.CostEstimate(
            flops=400_000_000, bytes_accessed=8_000_000, transcendentals=2_000_000
        ),
        name="token_stage",
    )(info, *args)


def scan_stage(
    info,
    mixed_ref,
    step_ref,
    proj_ref,
    enter_ref,
    start_ref,
    decay_ref,
    skip_ref,
    hidden_ref,
    gain_ref,
    out_w_hbm,
    middle_ref,
    normed_ref,
    final_ref,
    bc_wide,
    y_ref,
    ssm_b,
    out_w,
    w_sem,
):
    rows, inner = mixed_ref.shape
    width = col_block(inner)
    tiles = width // LANES
    rank = proj_ref.shape[1] - 2 * STATE
    fetch = pltpu.make_async_copy(out_w_hbm, out_w, w_sem)
    fetch.start()

    turned = jnp.transpose(proj_ref[:, rank : rank + 2 * STATE])
    for t in range(rows):
        bc_wide[t] = jnp.broadcast_to(turned[:, t : t + 1], (2 * STATE, LANES))
    final_ref[...] = jnp.zeros_like(final_ref)
    power = (lax.broadcasted_iota(jnp.int32, (8, LANES), 0) + 1).astype(jnp.float32)

    def wide_step(t, i, step, push, fade8, state, rates):
        b_low, b_high = bc_wide[t, 0:8], bc_wide[t, 8:16]
        c_low, c_high = bc_wide[t, 16:24], bc_wide[t, 24:32]
        outs, new = [], []
        for j in range(tiles):
            s_row, p_row, f_row = (
                jnp.broadcast_to(part[j][i : i + 1], (8, LANES)) for part in (step, push, fade8)
            )
            d_low = jnp.exp(s_row * rates[j])
            d_high = d_low * f_row
            low = d_low * state[2 * j] + b_low * p_row
            high = d_high * state[2 * j + 1] + b_high * p_row
            new += [low, high]
            outs.append(jnp.sum(c_low * low + c_high * high, axis=0, keepdims=True))
        return outs, tuple(new)

    def one_block(g, carry):
        base = pl.multiple_of(g * width, LANES)
        tile_cols = [pl.ds(pl.multiple_of(base + j * LANES, LANES), LANES) for j in range(tiles)]
        rates = [-decay_ref[:, c] * power for c in tile_cols]
        decays = [decay_ref[:, c] for c in tile_cols]

        def load(row, count):
            step = [step_ref[pl.ds(row, count), c] for c in tile_cols]
            push = [s * mixed_ref[pl.ds(row, count), c] for s, c in zip(step, tile_cols)]
            fade8 = [jnp.exp(-8.0 * (s * d)) for s, d in zip(step, decays)]
            return step, push, fade8

        def eight(block, state, limits=None):
            row = pl.multiple_of(block * 8, 8)
            step, push, fade8 = load(row, 8)
            kept = [[] for _ in range(tiles)]
            for i in range(8):
                outs, new = wide_step(row + i, i, step, push, fade8, state, rates)
                if limits is not None:
                    active = (row + i >= limits[0]) & (row + i < limits[1])
                    new = tuple(jnp.where(active, a, b) for a, b in zip(new, state))
                state = new
                for j in range(tiles):
                    kept[j].append(outs[j])
            for j in range(tiles):
                y = jnp.concatenate(kept[j], axis=0)
                if limits is not None:
                    at = row + lax.broadcasted_iota(jnp.int32, (8, LANES), 0)
                    y = jnp.where(
                        (at >= limits[0]) & (at < limits[1]), y, y_ref[pl.ds(row, 8), tile_cols[j]]
                    )
                y_ref[pl.ds(row, 8), tile_cols[j]] = y
            return state

        for r in range(final_ref.shape[0]):
            _, begin, end, new, ends = segment(info, r, rows)

            @pl.when(end > begin)
            def _():
                state = []
                for c in tile_cols:
                    for half in (pl.ds(0, 8), pl.ds(8, 8)):
                        old = enter_ref[half, c]
                        seed = start_ref[r, half, c].astype(jnp.float32)
                        state.append(jnp.where(new, seed, old))
                state = tuple(state)
                part = functools.partial(eight, limits=(begin, end))
                low, low_up, high = begin // 8, (begin + 7) // 8, end // 8
                state = lax.fori_loop(low, low_up, part, state)
                state = lax.fori_loop(low_up, jnp.maximum(high, low_up), eight, state)
                tail = jnp.where((high >= low_up) & (end % 8 > 0), high + 1, high)
                state = lax.fori_loop(high, tail, part, state)

                @pl.when(ends)
                def _():
                    for j, c in enumerate(tile_cols):
                        final_ref[r, pl.ds(0, 8), c] = state[2 * j]
                        final_ref[r, pl.ds(8, 8), c] = state[2 * j + 1]

        y = y_ref[:, pl.ds(base, width)]
        y = y + skip_ref[:, pl.ds(base, width)] * mixed_ref[:, pl.ds(base, width)]
        ssm_b[:, pl.ds(base, width)] = y.astype(jnp.bfloat16)
        return carry

    lax.fori_loop(0, inner // width, one_block, 0)
    fetch.wait()
    middle = hidden_ref[...].astype(jnp.float32)
    for first in range(0, inner, width):
        middle = middle + jnp.dot(
            ssm_b[:, first : first + width],
            out_w[first : first + width],
            preferred_element_type=jnp.float32,
        )
    middle_ref[...] = middle
    scale = lax.rsqrt(jnp.mean(middle * middle, axis=1, keepdims=True) + NORM_EPS)
    normed_ref[...] = (middle * scale * gain_ref[...]).astype(jnp.bfloat16)


def scan_call(info, args, out_w, rows, inner, model, requests):
    f32 = jnp.float32
    return pl.pallas_call(
        scan_stage,
        out_shape=(
            jax.ShapeDtypeStruct((rows, model), f32),
            jax.ShapeDtypeStruct((rows, model), jnp.bfloat16),
            jax.ShapeDtypeStruct((requests, STATE, inner), f32),
        ),
        in_specs=[sspec()] + [vspec()] * len(args) + [pl.BlockSpec(memory_space=pl.ANY)],
        out_specs=tuple([vspec()] * 3),
        scratch_shapes=[
            VMEM((rows, 2 * STATE, LANES), f32),
            VMEM((rows, inner), f32),
            VMEM((rows, inner), jnp.bfloat16),
            VMEM((inner, model), jnp.bfloat16),
            pltpu.SemaphoreType.DMA,
        ],
        compiler_params=pltpu.CompilerParams(vmem_limit_bytes=48 << 20),
        cost_estimate=pl.CostEstimate(
            flops=1_400_000_000, bytes_accessed=18_000_000, transcendentals=4_000_000
        ),
        name="scan_stage",
    )(info, *args, out_w)


def passed_along(block, axis, distance):
    devices = range(lax.axis_size(axis))
    route = [(i - distance, i) for i in devices if i - distance in devices]
    return lax.ppermute(block, axis, route)


def picked(array, chooser):
    return jnp.einsum("rj,jsc->rsc", chooser, array, precision=HIGHEST_PREC)


def shards(
    hidden_in,
    mamba_in,
    conv_weight,
    conv_bias,
    x_proj,
    dt_proj,
    dt_bias,
    decay_rate,
    skip_gain,
    out_proj,
    norm_gain,
    mlp_gate,
    mlp_up,
    mlp_down,
    cache_state,
    cache_edge,
    req_lengths,
    cont_flag,
    cache_source,
    owner_slot,
):
    rows, inner = mamba_in.shape[1:]
    model = hidden_in.shape[2]
    requests = req_lengths.shape[1]
    devices = lax.axis_size("seq")
    place = lax.axis_index("seq")
    info = jnp.concatenate(
        [
            req_lengths[0],
            cont_flag[0],
            cache_source[0],
            owner_slot[0],
            jnp.reshape(place * rows, (1,)).astype(jnp.int32),
        ]
    )
    bf16 = jnp.bfloat16
    states = lax.all_gather(cache_state[0, 0].astype(bf16), "seq")
    edges = lax.all_gather(cache_edge[0, 0], "seq")
    chooser = (
        cont_flag[0][:, None]
        * (cache_source[0][:, None] == jnp.arange(devices)[None, :]).astype(jnp.int32)
    ).astype(jnp.float32)
    start_state = picked(states.astype(jnp.float32), chooser)
    start_edge = picked(edges.astype(jnp.float32), chooser).astype(bf16)
    start_edge = start_edge.reshape(requests * EDGE, inner)
    start_edge = jnp.pad(start_edge, ((0, 16 - requests * EDGE), (0, 0)))
    halo = passed_along(mamba_in[0, rows - 16 :], "seq", 1)
    mixed, step, proj, end_state, step_sum, last_edge = token_call(
        info,
        (
            mamba_in[0],
            halo,
            start_edge,
            start_state,
            conv_weight,
            conv_bias[None],
            x_proj,
            dt_proj,
            dt_bias[None],
            decay_rate[None],
        ),
        rows,
        inner,
        x_proj.shape[1],
    )
    all_end = lax.all_gather(end_state, "seq")
    all_sum = lax.all_gather(step_sum[0], "seq")
    rates = (jnp.arange(STATE) + 1).astype(jnp.float32)[:, None] * decay_rate[None, :]
    enter = jnp.zeros_like(end_state)

    def lap(k, before):
        after = jnp.exp(-rates * all_sum[k][None]) * before + all_end[k]
        return jnp.where(k < place, after, before)

    enter = lax.fori_loop(0, devices, lap, enter)
    middle, normed, finals = scan_call(
        info,
        (
            mixed,
            step,
            proj,
            enter,
            start_state,
            decay_rate[None],
            skip_gain[None],
            hidden_in[0],
            norm_gain[None],
        ),
        out_proj,
        rows,
        inner,
        model,
        requests,
    )
    sums = jnp.concatenate([finals.reshape(requests * STATE, inner), last_edge], axis=0)
    sums = lax.psum(sums.astype(bf16), "seq")
    owned = (owner_slot[0] == place).astype(bf16)
    new_state = jnp.einsum("r,rsc->sc", owned, sums[: requests * STATE].reshape(finals.shape))
    last = sums[requests * STATE :][: requests * EDGE].reshape(requests, EDGE, inner)
    new_edge = jnp.einsum("r,rsc->sc", owned, last)
    piece = lax.all_gather(normed, "req", axis=0, tiled=True)
    gate_v = jnp.dot(piece, mlp_gate, preferred_element_type=jnp.float32)
    up_v = jnp.dot(piece, mlp_up, preferred_element_type=jnp.float32)
    hidden = (jax.nn.silu(gate_v) * up_v).astype(bf16)
    mlp_out = lax.psum_scatter(
        jnp.dot(hidden, mlp_down, preferred_element_type=jnp.float32).astype(bf16),
        "req",
        scatter_dimension=0,
        tiled=True,
    ).astype(jnp.float32)
    block_rows = (middle + mlp_out).astype(bf16)
    return (
        block_rows[None],
        new_state.astype(jnp.float32)[None, None],
        new_edge.astype(bf16)[None, None],
    )


def solution(mesh):
    grouped = P("req", "seq", None)
    slots = P("req", "seq", None, None)
    return jax.shard_map(
        shards,
        mesh=mesh,
        in_specs=(grouped, grouped)
        + (P(),) * 9
        + (P(None, "req"), P(None, "req"), P("req", None), slots, slots)
        + (P("req", None),) * 4,
        out_specs=(grouped, slots, slots),
        check_vma=False,
    )
```

profile of v0, /device:TPU:0, one launch (start us, length us, event | category | flops | bytes accessed | tf_op | source)
XLA Modules:
  0.0 383.3 jit_solution(16813767973188255079)
XLA Ops:
  7.3 1.6 convert_element_type.48
  9.0 1.5 slice_bitcast_fusion
  10.5 1.3 collective-permute-start
  13.3 1.3 broadcast_in_dim.35.dt_bias_ref
  14.6 26.9 %all-gather = bf16[32,1,3,3200]{3,2,1,0:T(4,128)(2,1)S(1)} all-gather(bf16[1,1,3,3200]{3,2,1,0:T(4,128)(2,1)} %param.37), channel_id=2, replica_groups=mesh['req'=4,'seq'=32] {'seq'}, dimensions={0}, use_global_device_ids=true | all-gather | bytes 633600 | tf_op jit(solution)/shard_map/all_gather | solution.py:419
  41.6 1.1 convolution_convert_fusion
  43.9 15.0 %all-gather.10.cloned.1.call-done = bf16[32,1,16,3200]{3,2,1,0:T(8,128)(2,1)} async-done(((bf16[1,1,16,3200]{3,2,1,0:T(8,128)(2,1)}), bf16[32,1,16,3200]{3,2,1,0:T(8,128)(2,1)}) %all-gather.10.cloned.1.call-update) | async-done | bytes 3276816 | tf_op jit(solution)/shard_map/all_gather | solution.py:418
  58.9 3.9 %fusion.5 = f32[4,16,3200]{2,0,1:T(4,128)S(1)} fusion(bf16[32,1,16,3200]{3,2,1,0:T(8,128)(2,1)} %all-gather.10.cloned.1.call-done, s32[4]{0:T(128)S(1)} %bitcast.67, s32[4]{0:T(128)S(1)} %bitcast.70), kind=kOutput, calls=%fused_computation.9 | convolution fusion | flops 78643584 | bytes 4096032 | tf_op jit(solution)/shard_map/rj,jsc->rsc/dot_general | solution.py:378
  64.4 9.3 %token_stage.1 = (f32[128,3200]{1,0:T(8,128)S(1)}, f32[128,3200]{1,0:T(8,128)S(1)}, f32[128,132]{1,0:T(8,128)S(1)}, f32[16,3200]{1,0:T(8,128)S(1)}, f32[1,3200]{1,0:T(1,128)S(1)}, /*index=5*/f32[16,3200]{1,0:T(8,128)S(1)}) custom-call(s32[17]{0:T(128)S(1)} %concatenate.7.info, bf16[128,3200]{1,0:T(8,128)(2,1)S(1)} %bitcast.58, ...), custom_call_target="tpu_custom_call" | custom-call | flops 400000000 | bytes 8000000 | tf_op jit(solution)/shard_map/token_stage/pallas_call | solution.py:191
  73.7 1.2 copy-done
  74.9 1.2 copy-done.2
  78.9 1.3 copy.58
  80.2 16.2 %copy.60.out_w_hbm = bf16[3200,1600]{1,0:T(8,128)(2,1)} copy(bf16[3200,1600]{0,1:T(8,128)(2,1)} %param.31) | data formatting | bytes 20480000 | tf_op args[9]
  96.5 24.5 %all-gather.3 = f32[32,1,3200]{2,1,0:T(1,128)S(1)} all-gather(f32[1,1,3200]{2,1,0:T(1,128)S(1)} %bitcast.59), channel_id=1, replica_groups=mesh['req'=4,'seq'=32] {'seq'}, dimensions={0}, use_global_device_ids=true | all-gather | bytes 422400 | tf_op jit(solution)/shard_map/all_gather | solution.py:448
  121.7 6.3 %all-gather.12.cloned.1.call-done = f32[512,3200]{1,0:T(8,128)} async-done(((f32[16,3200]{1,0:T(8,128)}), f32[512,3200]{1,0:T(8,128)}) %all-gather.12.cloned.1.call-update) | async-done | bytes 6553616 | tf_op jit(solution)/shard_map/all_gather | solution.py:447
  128.0 65.6 %while.16 = (s32[]{:T(128)}, f32[16,3200]{1,0:T(8,128)S(1)}, s32[]{:T(128)}, f32[32,3200]{1,0:T(8,128)}, f32[32,16,3200]{2,1,0:T(8,128)}, /*index=5*/f32[3200]{0:T(1024)S(1)}, f32[16]{0:T(128)S(1)}, s32[]{:T(128)}, s32[]{:T(128)}) while((s32[]{:T(128)}, f32[16,3200]{1,0:T(8,128)S(1)}, s32[]{:T(128)}, f32[32,3200]{1,0:T(8,128)}, ...), condition=%wide.region_1.2_spmd.clone, body=%wide.region_0.1_spmd.clone.sunk | while | flops 358404 | bytes 665793 | solution.py:456
  131.0 1.1 fusion.38
  133.0 1.1 fusion.38
  137.1 1.1 fusion.38
  139.2 1.1 fusion.38
  141.2 1.1 fusion.38
  143.3 1.1 fusion.38
  145.3 1.1 fusion.38
  147.4 1.1 fusion.38
  149.4 1.1 fusion.38
  151.5 1.1 fusion.38
  153.5 1.1 fusion.38
  157.7 1.1 fusion.38
  159.7 1.1 fusion.38
  163.8 1.1 fusion.38
  165.9 1.1 fusion.38
  170.0 1.1 fusion.38
  172.0 1.1 fusion.38
  176.1 1.1 fusion.38
  178.2 1.1 fusion.38
  180.2 1.1 fusion.38
  182.3 1.1 fusion.38
  184.3 1.1 fusion.38
  186.4 1.1 fusion.38
  188.4 1.1 fusion.38
  193.6 16.8 %scan_stage.1 = (f32[128,1600]{1,0:T(8,128)S(1)}, bf16[128,1600]{1,0:T(8,128)(2,1)}, f32[4,16,3200]{2,1,0:T(8,128)S(1)}) custom-call(s32[17]{0:T(128)S(1)} %concatenate.7.info, f32[128,3200]{1,0:T(8,128)S(1)} %copy-done.1, f32[128,3200]{1,0:T(8,128)} %copy-done.2, f32[128,132]{1,0:T(8,128)S(1)} %get-tuple-element.163.proj_ref, ...), custom_call_target="tpu_custom_call" | custom-call | flops 1400000000 | bytes 18000000 | tf_op jit(solution)/shard_map/scan_stage/pallas_call | solution.py:347
  212.4 1.2 convert.8
  214.7 24.7 %all-gather.8.cloned.1.call-done = bf16[512,1600]{1,0:T(8,128)(2,1)} async-done(((bf16[128,1600]{1,0:T(8,128)(2,1)}), bf16[512,1600]{1,0:T(8,128)(2,1)}) %all-gather.8.cloned.1.call-update) | async-done | bytes 1638416 | tf_op jit(solution)/shard_map/all_gather | solution.py:482
  239.4 7.2 %fusion.31 = f32[512,1376]{0,1:T(8,128)} fusion(bf16[512,1600]{1,0:T(8,128)(2,1)} %all-gather.8.cloned.1.call-done, bf16[1600,1376]{1,0:T(8,128)(2,1)} %param.33), kind=kOutput, calls=%fused_computation.45 | convolution fusion | flops 2254438400 | bytes 8859648 | tf_op jit(solution)/shard_map/dot_general | solution.py:483
  246.7 10.1 %convolution_convert_fusion.1 = bf16[512,1600]{0,1:T(8,128)(2,1)S(1)} fusion(bf16[1376,1600]{0,1:T(8,128)(2,1)} %param.35, bf16[512,1600]{1,0:T(8,128)(2,1)S(1)} %copy-done.25, bf16[1600,1376]{1,0:T(8,128)(2,1)} %param.34, f32[512,1376]{0,1:T(8,128)} %fusion.31), kind=kOutput, calls=%fused_computation.13 | convolution fusion | flops 4513923072 | bytes 14901248 | tf_op jit(solution)/shard_map/dot_general | solution.py:487
  256.7 2.4 copy.61
  259.2 87.1 %all-reduce.3.cloned.1.call-done = bf16[80,3200]{1,0:T(8,128)(2,1)} async-done(((bf16[80,3200]{1,0:T(8,128)(2,1)}), bf16[80,3200]{1,0:T(8,128)(2,1)}) %all-reduce.3.cloned.1.call-update) | async-done | bytes 512016 | tf_op jit(solution)/shard_map/psum | solution.py:477
  350.1 24.6 %reduce-scatter.2.cloned.1.call-done = bf16[128,1600]{1,0:T(8,128)(2,1)} async-done(((bf16[512,1600]{1,0:T(8,128)(2,1)}), bf16[128,1600]{1,0:T(8,128)(2,1)}) %reduce-scatter.2.cloned.1.call-update) | async-done | bytes 409616 | tf_op jit(solution)/shard_map/reduce_scatter | solution.py:486
  (125 shorter events, 55.7 us)
Async XLA Ops:
  7.2 36.7 %copy-start.21 = (s32[1,4]{1,0:T(1,128)S(1)}, s32[1,4]{1,0:T(1,128)}, u32[]{:S(2)}) copy-start(s32[1,4]{1,0:T(1,128)} %param.40) | copy-start | bytes 52
  7.2 36.6 %copy-start.20 = (s32[1,4]{1,0:T(1,128)S(1)}, s32[1,4]{1,0:T(1,128)}, u32[]{:S(2)}) copy-start(s32[1,4]{1,0:T(1,128)} %param.39) | copy-start | bytes 52
  7.2 35.6 %copy-start.17 = (bf16[3200,132]{0,1:T(8,128)(2,1)S(1)}, bf16[3200,132]{0,1:T(8,128)(2,1)}, u32[]{:S(2)}) copy-start(bf16[3200,132]{0,1:T(8,128)(2,1)} %param.26) | copy-start | bytes 2534404
  7.2 36.6 %copy-start.23 = (s32[1,4]{1,0:T(1,128)S(1)}, s32[1,4]{1,0:T(1,128)}, u32[]{:S(2)}) copy-start(s32[1,4]{1,0:T(1,128)} %param.41) | copy-start | bytes 52
  7.2 36.6 %copy-start.22 = (s32[1,4]{1,0:T(1,128)S(1)}, s32[1,4]{1,0:T(1,128)}, u32[]{:S(2)}) copy-start(s32[1,4]{1,0:T(1,128)} %param.38) | copy-start | bytes 52
  7.2 51.7 %all-gather.10.cloned.1.call-start = ((), (), s32[]{:S(2)}) async-start(), calls=%async_computation.4 | async-start | bytes 3379200 | tf_op jit(solution)/shard_map/all_gather | solution.py:418
  8.9 119.1 %all-gather.12.cloned.1.call-start = ((), (), s32[]{:S(2)}) async-start(), calls=%async_computation.5 | async-start | bytes 6758400 | tf_op jit(solution)/shard_map/all_gather | solution.py:447
  10.5 52.3 %collective-permute-start = (bf16[16,3200]{1,0:T(8,128)(2,1)}, bf16[16,3200]{1,0:T(8,128)(2,1)S(1)}, u32[]{:S(2)}, u32[]{:S(2)}) collective-permute-start(bf16[16,3200]{1,0:T(8,128)(2,1)} %slice_bitcast_fusion), channel_id=1, source_target_pairs={{0,1},{1,2},{2,3},{3,4},{4,5},{5,6},{6,7},{7,8},{8,9},{9,10},{10,1... | collective-permute-start | bytes 307208 | tf_op jit(solution)/shard_map/ppermute | solution.py:374
  43.9 19.6 %copy-start.3 = (bf16[1,128,3200]{2,1,0:T(8,128)(2,1)S(1)}, bf16[1,128,3200]{2,1,0:T(8,128)(2,1)}, u32[]{:S(2)}) copy-start(bf16[1,128,3200]{2,1,0:T(8,128)(2,1)} %param.23) | copy-start | bytes 2457604
  58.9 4.6 %copy-start.7 = (bf16[100,3200]{1,0:T(8,128)(2,1)S(1)}, bf16[100,3200]{1,0:T(8,128)(2,1)}, u32[]{:S(2)}) copy-start(bf16[100,3200]{1,0:T(8,128)(2,1)} %dt_proj_ref.1) | copy-start | bytes 1920004
  58.9 4.6 %copy-start.13 = (f32[1,3200]{1,0:T(1,128)S(1)}, f32[1,3200]{1,0:T(1,128)}, u32[]{:S(2)}) copy-start(f32[1,3200]{1,0:T(1,128)} %broadcast_in_dim.35.dt_bias_ref) | copy-start | bytes 38404
  58.9 4.6 %copy-start.14 = (f32[4,3200]{1,0:T(4,128)S(1)}, f32[4,3200]{1,0:T(4,128)}, u32[]{:S(2)}) copy-start(f32[4,3200]{1,0:T(4,128)} %conv_w_ref.1) | copy-start | bytes 153604
  62.8 15.4 %copy-start.19 = (f32[1600]{0:T(1024)S(1)}, f32[1600]{0:T(1024)}, u32[]{:S(2)}) copy-start(f32[1600]{0:T(1024)} %param.32) | copy-start | bytes 19204
  62.9 0.6 copy-start.11
  63.5 0.9 copy-start.12
  73.7 1.2 copy-start
  74.9 1.2 copy-start.2
  76.1 0.7 copy-start.8
  76.8 0.7 copy-start.10
  77.5 0.6 copy-start.15
  78.1 161.3 %all-gather.8.cloned.1.call-start = ((), (), s32[]{:S(2)}) async-start(), calls=%async_computation.1 | async-start | bytes 2129920 | tf_op jit(solution)/shard_map/all_gather | solution.py:482
  80.2 16.3 %copy-start.16 = (f32[1,3200]{1,0:T(1,128)S(1)}, f32[1,3200]{1,0:T(1,128)}, u32[]{:S(2)}) copy-start(f32[1,3200]{1,0:T(1,128)} %copy-done.15) | copy-start | bytes 38404
  80.2 47.8 %copy-start.18 = (f32[3200]{0:T(1024)S(1)}, f32[3200]{0:T(1024)}, u32[]{:S(2)}) copy-start(f32[3200]{0:T(1024)} %param.29) | copy-start | bytes 38404
  96.4 97.2 %copy-start.1 = (f32[128,3200]{1,0:T(8,128)S(1)}, f32[128,3200]{1,0:T(8,128)}, u32[]{:S(2)}) copy-start(f32[128,3200]{1,0:T(8,128)} %copy-done) | copy-start | bytes 4915204
  193.6 18.7 %copy-start.9 = (f32[16,3200]{1,0:T(8,128)S(1)}, f32[16,3200]{1,0:T(8,128)}, u32[]{:S(2)}) copy-start(f32[16,3200]{1,0:T(8,128)} %copy-done.8) | copy-start | bytes 614404
  210.4 0.9 copy-start.4
  211.4 0.9 copy-start.6
  212.3 133.9 %all-reduce.3.cloned.1.call-start = ((), (), s32[]{:S(2)}) async-start(), calls=%async_computation.3 | async-start | bytes 1024000 | tf_op jit(solution)/shard_map/psum | solution.py:477
  214.4 160.2 %reduce-scatter.2.cloned.1.call-start = ((), (), s32[]{:S(2)}) async-start(), calls=%async_computation.2 | async-start | bytes 2129920 | tf_op jit(solution)/shard_map/reduce_scatter | solution.py:486
  239.4 7.2 %copy-start.25 = (bf16[512,1600]{1,0:T(8,128)(2,1)S(1)}, bf16[512,1600]{1,0:T(8,128)(2,1)}, u32[]{:S(2)}) copy-start(bf16[512,1600]{1,0:T(8,128)(2,1)} %all-gather.8.cloned.1.call-done) | copy-start | bytes 4915204
  256.7 90.5 %copy-start.24 = (s32[1,4]{1,0:T(1,128)S(1)}, s32[1,4]{1,0:T(1,128)}, u32[]{:S(2)}) copy-start(s32[1,4]{1,0:T(1,128)} %param.41) | copy-start | bytes 52
  259.1 115.6 %copy-start.5 = (f32[128,1600]{1,0:T(8,128)S(1)}, f32[128,1600]{1,0:T(8,128)}, u32[]{:S(2)}) copy-start(f32[128,1600]{1,0:T(8,128)} %copy-done.4) | copy-start | bytes 2457604
Sparse Core Ops, SparseCore 0:
  11.0 47.9 all-gather.9
  78.2 49.7 all-gather.11
  212.4 26.9 all-gather.7
  242.5 103.6 all-reduce.2
  348.6 26.0 reduce-scatter.1
where the time goes:
time: 387 us; the launch traced here: 383 us
  waiting for transfers between devices  158 us (41%)
  local copies, waits for them, and re-layouts  68.4 us (18%)
  blocking collectives  51.4 us (13%)
  other arithmetic  40.2 us (10%)
  Pallas kernels  26.1 us (7%)
  matrix products  22.8 us (6%)
  between operations  14.1 us (4%)
    psum x1, waiting for transfers between devices, shards(): sums = lax.psum(sums.astype(bf16), 'seq')  87.1 us
    select_n x32, other arithmetic, lap(): return jnp.where(k < place, after, before)  34.8 us
    dynamic_slice x32, local copies, waits for them, and re-layouts, lap(): after = jnp.exp(-rates * all_sum[k][None]) * before + all_end[k]  30.1 us
    unnamed x57, local copies, waits for them, and re-layouts  28 us
    all_gather x1, blocking collectives, shards(): edges = lax.all_gather(cache_edge[0, 0], 'seq')  26.9 us
    all_gather x1, waiting for transfers between devices, shards(): piece = lax.all_gather(normed, 'req', axis=0, tiled=True)  24.7 us
    reduce_scatter x1, waiting for transfers between devices, shards(): lax.psum_scatter(jnp.dot(hidden, mlp_down, preferred_element_type=jnp.flo...  24.6 us
    all_gather x1, blocking collectives, shards(): all_sum = lax.all_gather(step_sum[0], 'seq')  24.5 us
  transfers between devices with their start and end apart: 6, of which 5 were waited for; matrix products, arithmetic and copies ran while one was open for 14% of the time, Pallas kernels for 0%

commit v1 on v0

--- a/solution.py
+++ b/solution.py
@@ -27,6 +27,177 @@
 
 def col_block(width):
     return 640 if width % 640 == 0 else LANES
+
+
+MESH_ID = pl.DeviceIdType.MESH
+
+
+def layout_of(devices):
+    depth = 4 if devices >= 32 else 2
+    return devices // (2 * depth), depth
+
+
+def half_width(inner):
+    return -(-inner // (2 * LANES)) * LANES
+
+
+def near_devices(devices):
+    across, depth = layout_of(devices)
+    me = lax.axis_index("seq")
+    core, z, x = me % 2, (me // 2) % depth, me // (2 * depth)
+    partner = me + 1 - 2 * core
+    z_peers = [x * 2 * depth + ((z + d) % depth) * 2 + core for d in range(1, depth)]
+    x_peers = [((x + d) % across) * 2 * depth + z * 2 + core for d in range(1, across)]
+    return me, core, z, x, partner, z_peers, x_peers
+
+
+def my_lanes(core, inner):
+    half = half_width(inner)
+    return pl.ds(pl.multiple_of(core * (inner - half), LANES), half)
+
+
+def send(src, dst, sems, index, peer):
+    return pltpu.make_async_remote_copy(
+        src_ref=src,
+        dst_ref=dst,
+        send_sem=sems.at[0, index],
+        recv_sem=sems.at[1, index],
+        device_id={"seq": peer},
+        device_id_type=MESH_ID,
+    )
+
+
+def greet(axis_peers):
+    barrier = pltpu.get_barrier_semaphore()
+    for axis, peer in axis_peers:
+        pl.semaphore_signal(barrier, inc=1, device_id={axis: peer}, device_id_type=MESH_ID)
+    pl.semaphore_wait(barrier, len(axis_peers))
+
+
+class Spread:
+    def __init__(self, devices, inner, count, split, refs):
+        self.devices, self.inner, self.count, self.split = devices, inner, count, split
+        self.across, self.depth = layout_of(devices)
+        self.part = count // self.depth if split else count
+        (
+            self.mine,
+            self.from_core,
+            self.acc,
+            self.from_z,
+            self.from_x,
+            self.from_z2,
+            self.other,
+            self.sems,
+        ) = refs
+        _, self.core, self.z, self.x, self.partner, self.z_peers, self.x_peers = near_devices(
+            devices
+        )
+        self.lanes = my_lanes(self.core, inner)
+        self.far_lanes = my_lanes(1 - self.core, inner)
+        self.copies = []
+
+    @staticmethod
+    def scratch(devices, inner, count, split):
+        across, depth = layout_of(devices)
+        part = count // depth if split else count
+        half = half_width(inner)
+        b = jnp.bfloat16
+        return [
+            VMEM((count, 16, inner), b),
+            VMEM((count, 16, half), b),
+            VMEM((count, 16, half), b),
+            VMEM((depth - 1, part, 16, half), b),
+            VMEM((across - 1, part, 16, half), b),
+            VMEM((depth - 1, part, 16, half), b),
+            VMEM((count, 16, half), b),
+            pltpu.SemaphoreType.DMA((2, 2 + 2 * (depth - 1) + (across - 1))),
+        ]
+
+    def own_part(self, shift=0):
+        if not self.split:
+            return pl.ds(0, self.part)
+        return pl.ds(((self.z + shift) % self.depth) * self.part, self.part)
+
+    def begin(self, copies):
+        self.copies = copies
+        for copy in copies:
+            copy.start()
+
+    def end(self):
+        for copy in self.copies:
+            copy.wait()
+
+    def start_core(self):
+        self.begin(
+            [send(self.mine.at[:, :, self.far_lanes], self.from_core, self.sems, 0, self.partner)]
+        )
+
+    def finish_core(self):
+        self.end()
+        total = self.mine[:, :, self.lanes].astype(jnp.float32) + self.from_core[...].astype(
+            jnp.float32
+        )
+        self.acc[...] = total.astype(jnp.bfloat16)
+
+    def start_z(self):
+        self.begin(
+            [
+                send(self.acc.at[self.own_part(d + 1)], self.from_z.at[d], self.sems, 1 + d, peer)
+                for d, peer in enumerate(self.z_peers)
+            ]
+        )
+
+    def finish_z(self):
+        self.end()
+        here = self.own_part()
+        total = self.acc[here].astype(jnp.float32)
+        for d in range(self.depth - 1):
+            total = total + self.from_z[d].astype(jnp.float32)
+        self.acc[here] = total.astype(jnp.bfloat16)
+
+    def start_x(self):
+        base = self.depth
+        self.begin(
+            [
+                send(self.acc.at[self.own_part()], self.from_x.at[d], self.sems, base + d, peer)
+                for d, peer in enumerate(self.x_peers)
+            ]
+        )
+
+    def finish_x(self):
+        self.end()
+        here = self.own_part()
+        total = self.acc[here].astype(jnp.float32)
+        for d in range(self.across - 1):
+            total = total + self.from_x[d].astype(jnp.float32)
+        self.acc[here] = total.astype(jnp.bfloat16)
+
+    def start_z2(self):
+        if not self.split:
+            return
+        base = self.depth + self.across - 1
+        self.begin(
+            [
+                send(self.acc.at[self.own_part()], self.from_z2.at[d], self.sems, base + d, peer)
+                for d, peer in enumerate(self.z_peers)
+            ]
+        )
+
+    def finish_z2(self):
+        if not self.split:
+            return
+        self.end()
+        for d in range(self.depth - 1):
+            self.acc[self.own_part(-(d + 1))] = self.from_z2[d]
+
+    def start_core2(self):
+        last = 2 * (self.depth - 1) + self.across
+        self.begin([send(self.acc, self.other, self.sems, last, self.partner)])
+
+    def finish_core2(self, out_ref):
+        self.end()
+        out_ref[:, :, self.lanes] = self.acc[...]
+        out_ref[:, :, self.far_lanes] = self.other[...]
 
 
 def segment(info, r, rows):
@@ -42,12 +213,12 @@
     return begin, low, high, fresh, ends
 
 
-def token_stage(
+def front_stage(
+    devices,
     info,
     x_ref,
-    halo_ref,
-    edge_ref,
-    start_ref,
+    cache_ref,
+    cache_edge_ref,
     conv_w_ref,
     conv_b_ref,
     x_proj_ref,
@@ -57,20 +228,71 @@
     mixed_ref,
     step_ref,
     proj_ref,
-    end_ref,
-    sum_ref,
+    enter_ref,
     last_edge_ref,
+    start_ref,
     ext,
     mixed_b,
     suffix,
     b_wide,
+    halo_ref,
+    edge3_ref,
+    end_ref,
+    sum_ref,
+    halo_sems,
+    pair_h,
+    pair_s,
+    own_h,
+    own_s,
+    z_h,
+    z_s,
+    x_h,
+    x_s,
+    half_out,
+    half_in,
+    pre_sems,
+    *spread_refs,
 ):
     rows, inner = x_ref.shape
+    requests = start_ref.shape[0]
+    me, core, z, x, partner, z_peers, x_peers = near_devices(devices)
+    after, before = (me + 1) % devices, (me + devices - 1) % devices
+    greet([("seq", p) for p in [partner, after, before] + z_peers + x_peers])
+    halo_copy = send(x_ref.at[pl.ds(rows - 16, 16)], halo_ref, halo_sems, 0, after)
+    halo_copy.start()
+    per = len(Spread.scratch(devices, inner, 1, False))
+    edge_sum = Spread(devices, inner, 1, False, spread_refs[:per])
+    state_sum = Spread(devices, inner, requests, True, spread_refs[per:])
+    spot = lax.broadcasted_iota(jnp.int32, (16, inner), 0)
+    edge_rows = cache_edge_ref[...].astype(jnp.float32)
+    placed = jnp.zeros((16, inner), jnp.float32)
+    for r in range(requests):
+        take = (info[8 + r] == me) & (info[4 + r] > 0)
+        for j in range(EDGE):
+            placed = jnp.where((spot == r * EDGE + j) & take, edge_rows[j : j + 1], placed)
+    edge_sum.mine[0] = placed.astype(jnp.bfloat16)
+    edge_sum.start_core()
+    for r in range(requests):
+        take = (info[8 + r] == me) & (info[4 + r] > 0)
+        state_sum.mine[r] = jnp.where(take, cache_ref[...], 0.0).astype(jnp.bfloat16)
+    state_sum.start_core()
+    ext[pl.ds(16, rows), :] = x_ref[...].astype(jnp.float32)
+    edge_sum.finish_core()
+    edge_sum.start_z()
+    state_sum.finish_core()
+    state_sum.start_z()
+    edge_sum.finish_z()
+    edge_sum.start_x()
+    state_sum.finish_z()
+    state_sum.start_x()
+    edge_sum.finish_x()
+    edge_sum.start_core2()
+    edge_sum.finish_core2(edge3_ref)
+    edge_ref = edge3_ref.at[0]
+    halo_copy.wait()
     width = col_block(inner)
     rank = dt_proj_ref.shape[0]
     ext[pl.ds(0, 16), :] = halo_ref[...].astype(jnp.float32)
-    ext[pl.ds(16, rows), :] = x_ref[...].astype(jnp.float32)
-    requests = start_ref.shape[0]
     first_pos = info[16]
     position = first_pos + lax.broadcasted_iota(jnp.int32, (rows, LANES), 0)
     marks = [segment(info, r, rows) for r in range(requests)]
@@ -109,7 +331,14 @@
         mixed_b[:, cols] = mixed
         mixed_ref[:, cols] = mixed.astype(jnp.float32)
 
-    proj = jnp.dot(mixed_b[...], x_proj_ref[...], preferred_element_type=jnp.float32)
+    proj = lax.dot_general(
+        mixed_b[...],
+        x_proj_ref[...],
+        (((1,), (1,)), ((), ())),
+        preferred_element_type=jnp.float32,
+    )
+    state_sum.finish_x()
+    state_sum.start_z2()
     proj_ref[...] = proj
     for s in range(STATE):
         b_wide[s] = jnp.broadcast_to(proj[:, rank + s : rank + s + 1], (rows, LANES))
@@ -134,6 +363,9 @@
         )
         suffix[:, cols] = after
 
+    state_sum.finish_z2()
+    state_sum.start_core2()
+    state_sum.finish_core2(start_ref)
     starts_here = (last_begin >= first_pos).astype(jnp.int32)
     flag = jnp.full((1, LANES), starts_here, jnp.int32).astype(jnp.float32)
     power = (lax.broadcasted_iota(jnp.int32, (STATE, LANES), 0) + 1).astype(jnp.float32)
@@ -160,6 +392,102 @@
         return carry
 
     lax.fori_loop(0, inner // LANES, one_tile, 0)
+    power16 = (lax.broadcasted_iota(jnp.int32, (STATE, LANES), 0) + 1).astype(jnp.float32)
+    half = half_width(inner)
+    tiles = half // LANES
+    base = core * (inner - half)
+    own_h[...] = end_ref[...].astype(jnp.bfloat16)
+    for j in range(inner // LANES):
+        own_s[pl.ds(j, 1), :] = sum_ref[:, pl.ds(j * LANES, LANES)]
+    pair = [
+        send(own_h, pair_h, pre_sems, 0, partner),
+        send(own_s, pair_s, pre_sems, 1, partner),
+    ]
+    for copy in pair:
+        copy.start()
+    across, depth = layout_of(devices)
+    first_core = core == 0
+
+    def lane(j):
+        return pl.ds(pl.multiple_of(base + j * LANES, LANES), LANES)
+
+    def f32(value):
+        return value.astype(jnp.float32)
+
+    for copy in pair:
+        copy.wait()
+    z_sum = []
+    for j in range(tiles):
+        rate = decay_ref[:, lane(j)] * power16
+        mine, theirs = own_h[:, lane(j)], pair_h[:, lane(j)]
+        shift = (inner - half) // LANES
+        s_mine = jnp.where(first_core, own_s[j : j + 1], own_s[j + shift : j + shift + 1])
+        s_pair = jnp.where(first_core, pair_s[j : j + 1], pair_s[j + shift : j + shift + 1])
+        h0 = f32(jnp.where(first_core, f32(mine), f32(theirs)))
+        h1 = f32(jnp.where(first_core, f32(theirs), f32(mine)))
+        s1 = jnp.where(first_core, s_pair, s_mine)
+        z_h[0, :, pl.ds(j * LANES, LANES)] = (jnp.exp(-rate * s1) * h0 + h1).astype(jnp.bfloat16)
+        z_s[0, pl.ds(j, 1), :] = s_mine + s_pair
+    copies = []
+    for d, peer in enumerate(z_peers):
+        copies.append(send(z_h.at[0], z_h.at[d + 1], pre_sems, 2 + 2 * d, peer))
+        copies.append(send(z_s.at[0], z_s.at[d + 1], pre_sems, 3 + 2 * d, peer))
+    for copy in copies:
+        copy.start()
+    for copy in copies:
+        copy.wait()
+    prefix = []
+    for j in range(tiles):
+        cols = pl.ds(j * LANES, LANES)
+        rate = decay_ref[:, lane(j)] * power16
+        total = jnp.zeros((STATE, LANES), jnp.float32)
+        part = jnp.zeros((STATE, LANES), jnp.float32)
+        total_s = jnp.zeros((1, LANES), jnp.float32)
+        part_s = jnp.zeros((1, LANES), jnp.float32)
+        for k in range(depth):
+            slot = (z - k + depth) % depth
+            s_k = z_s[slot, pl.ds(j, 1), :]
+            h_k = f32(z_h[slot, :, cols])
+            fade = jnp.exp(-rate * s_k)
+            total = fade * total + h_k
+            part = jnp.where(k < z, fade * part + h_k, part)
+            total_s = total_s + s_k
+            part_s = jnp.where(k < z, part_s + s_k, part_s)
+        x_h[0, :, cols] = total.astype(jnp.bfloat16)
+        x_s[0, pl.ds(j, 1), :] = total_s
+        prefix.append((part, part_s))
+    copies = []
+    first = 2 + 2 * (depth - 1)
+    for d, peer in enumerate(x_peers):
+        copies.append(send(x_h.at[0], x_h.at[d + 1], pre_sems, first + 2 * d, peer))
+        copies.append(send(x_s.at[0], x_s.at[d + 1], pre_sems, first + 1 + 2 * d, peer))
+    for copy in copies:
+        copy.start()
+    for copy in copies:
+        copy.wait()
+    for j in range(tiles):
+        cols = pl.ds(j * LANES, LANES)
+        rate = decay_ref[:, lane(j)] * power16
+        part = jnp.zeros((STATE, LANES), jnp.float32)
+        for k in range(across):
+            slot = (x - k + across) % across
+            value = jnp.exp(-rate * x_s[slot, pl.ds(j, 1), :]) * part + f32(x_h[slot, :, cols])
+            part = jnp.where(k < x, value, part)
+        inner_part, inner_s = prefix[j]
+        half_out[:, cols] = jnp.exp(-rate * inner_s) * part + inner_part
+    last = first + 2 * (across - 1)
+    swap = send(half_out, half_in, pre_sems, last, partner)
+    swap.start()
+    swap.wait()
+    enter_ref[:, my_lanes(core, inner)] = half_out[...]
+    enter_ref[:, my_lanes(1 - core, inner)] = half_in[...]
+    for j in range(inner // LANES):
+        cols = pl.ds(j * LANES, LANES)
+        rate = decay_ref[:, cols] * power16
+        chip = enter_ref[:, cols]
+        second = jnp.exp(-rate * pair_s[j : j + 1]) * chip + f32(pair_h[:, cols])
+        enter_ref[:, cols] = jnp.where(first_core, chip, second)
+
     row_of = lax.broadcasted_iota(jnp.int32, (16, LANES), 0)
     from_of = lax.broadcasted_iota(jnp.int32, (16, LANES), 1)
     near_at = jnp.full((16, LANES), -1, jnp.int32)
@@ -186,31 +514,54 @@
         )
 
 
-def token_call(info, args, rows, inner, proj_width):
-    f32 = jnp.float32
+def front_call(devices, info, args, rows, inner, proj_width, requests):
+    f32, bf16 = jnp.float32, jnp.bfloat16
+    across, depth = layout_of(devices)
+    half = half_width(inner)
+    s_rows = -(-(inner // LANES) // 8) * 8
     return pl.pallas_call(
-        token_stage,
+        functools.partial(front_stage, devices),
         out_shape=(
             jax.ShapeDtypeStruct((rows, inner), f32),
             jax.ShapeDtypeStruct((rows, inner), f32),
             jax.ShapeDtypeStruct((rows, proj_width), f32),
             jax.ShapeDtypeStruct((STATE, inner), f32),
-            jax.ShapeDtypeStruct((1, inner), f32),
             jax.ShapeDtypeStruct((16, inner), f32),
+            jax.ShapeDtypeStruct((requests, STATE, inner), bf16),
         ),
         in_specs=[sspec()] + [vspec()] * len(args),
         out_specs=tuple([vspec()] * 6),
         scratch_shapes=[
             VMEM((rows + 16, inner), f32),
-            VMEM((rows, inner), jnp.bfloat16),
+            VMEM((rows, inner), bf16),
             VMEM((rows, inner), f32),
             VMEM((STATE, rows, LANES), f32),
-        ],
-        compiler_params=pltpu.CompilerParams(vmem_limit_bytes=40 << 20),
+            VMEM((16, inner), bf16),
+            VMEM((1, 16, inner), bf16),
+            VMEM((STATE, inner), f32),
+            VMEM((1, inner), f32),
+            pltpu.SemaphoreType.DMA((2, 1)),
+            VMEM((STATE, inner), bf16),
+            VMEM((s_rows, LANES), f32),
+            VMEM((STATE, inner), bf16),
+            VMEM((s_rows, LANES), f32),
+            VMEM((depth, STATE, half), bf16),
+            VMEM((depth, 16, LANES), f32),
+            VMEM((across, STATE, half), bf16),
+            VMEM((across, 16, LANES), f32),
+            VMEM((STATE, half), f32),
+            VMEM((STATE, half), f32),
+            pltpu.SemaphoreType.DMA((2, 3 + 2 * (depth + across - 2))),
+        ]
+        + Spread.scratch(devices, inner, 1, False)
+        + Spread.scratch(devices, inner, requests, True),
+        compiler_params=pltpu.CompilerParams(
+            vmem_limit_bytes=48 << 20, collective_id=0, has_side_effects=True
+        ),
         cost_estimate=pl.CostEstimate(
             flops=400_000_000, bytes_accessed=8_000_000, transcendentals=2_000_000
         ),
-        name="token_stage",
+        name="front_stage",
     )(info, *args)
 
 
@@ -330,11 +681,12 @@
 
     lax.fori_loop(0, inner // width, one_block, 0)
     fetch.wait()
-    middle = hidden_ref[...].astype(jnp.float32)
+    middle = jnp.transpose(hidden_ref[...].astype(jnp.float32))
     for first in range(0, inner, width):
-        middle = middle + jnp.dot(
+        middle = middle + lax.dot_general(
             ssm_b[:, first : first + width],
-            out_w[first : first + width],
+            out_w[:, first : first + width],
+            (((1,), (1,)), ((), ())),
             preferred_element_type=jnp.float32,
         )
     middle_ref[...] = middle
@@ -357,7 +709,7 @@
             VMEM((rows, 2 * STATE, LANES), f32),
             VMEM((rows, inner), f32),
             VMEM((rows, inner), jnp.bfloat16),
-            VMEM((inner, model), jnp.bfloat16),
+            VMEM((model, inner), jnp.bfloat16),
             pltpu.SemaphoreType.DMA,
         ],
         compiler_params=pltpu.CompilerParams(vmem_limit_bytes=48 << 20),
@@ -368,14 +720,197 @@
     )(info, *args, out_w)
 
 
-def passed_along(block, axis, distance):
-    devices = range(lax.axis_size(axis))
-    route = [(i - distance, i) for i in devices if i - distance in devices]
-    return lax.ppermute(block, axis, route)
-
-
-def picked(array, chooser):
-    return jnp.einsum("rj,jsc->rsc", chooser, array, precision=HIGHEST_PREC)
+def mlp_stage(
+    devices,
+    info,
+    normed_ref,
+    middle_ref,
+    final_ref,
+    last_edge_ref,
+    gate_hbm,
+    up_hbm,
+    down_hbm,
+    out_ref,
+    new_state_ref,
+    new_edge_ref,
+    gate_w,
+    up_w,
+    down_w,
+    w_sems,
+    near,
+    far,
+    near_out,
+    far_out,
+    own_out,
+    low_in,
+    high_in,
+    far_in,
+    ring_sems,
+    full,
+    *spread_refs,
+):
+    rows, model = normed_ref.shape
+    half = rows // 2
+    inner = final_ref.shape[2]
+    requests = final_ref.shape[0]
+    me, _, _, _, partner, z_peers, x_peers = near_devices(devices)
+    ring = lax.axis_size("req")
+    here = lax.axis_index("req")
+    above, below = (here + 1) % ring, (here + ring - 1) % ring
+    fetches = [
+        pltpu.make_async_copy(gate_hbm, gate_w, w_sems.at[0]),
+        pltpu.make_async_copy(up_hbm, up_w, w_sems.at[1]),
+        pltpu.make_async_copy(down_hbm, down_w, w_sems.at[2]),
+    ]
+    for copy in fetches:
+        copy.start()
+    greet(
+        [("req", above), ("req", below)] + [("seq", p) for p in [partner] + z_peers + x_peers]
+    )
+
+    def hop(src, dst, index, peer):
+        return pltpu.make_async_remote_copy(
+            src_ref=src,
+            dst_ref=dst,
+            send_sem=ring_sems.at[0, index],
+            recv_sem=ring_sems.at[1, index],
+            device_id={"req": peer},
+            device_id_type=MESH_ID,
+        )
+
+    first, second = pl.ds(0, half), pl.ds(half, half)
+    third, fourth = pl.ds(2 * half, half), pl.ds(3 * half, half)
+    up_a = hop(normed_ref.at[first], near.at[first], 0, above)
+    down_b = hop(normed_ref.at[second], near.at[fourth], 1, below)
+    up_a.start()
+    down_b.start()
+    finals = Spread(devices, inner, requests + requests, True, spread_refs)
+    for r in range(requests):
+        finals.mine[2 * r] = final_ref[r].astype(jnp.bfloat16)
+        edges = last_edge_ref[pl.ds(r * EDGE, EDGE), :]
+        rest = jnp.zeros((16 - EDGE, inner), jnp.float32)
+        finals.mine[2 * r + 1] = jnp.concatenate([edges, rest], axis=0).astype(jnp.bfloat16)
+    finals.start_core()
+
+    def hidden_units(value):
+        gate = jnp.dot(value, gate_w[...], preferred_element_type=jnp.float32)
+        up = jnp.dot(value, up_w[...], preferred_element_type=jnp.float32)
+        hidden = (gate / (1.0 + jnp.exp(-gate)) * up).astype(jnp.bfloat16)
+        return lax.dot_general(
+            hidden, down_w[...], (((1,), (1,)), ((), ())), preferred_element_type=jnp.float32
+        )
+
+    for copy in fetches:
+        copy.wait()
+    up_a.wait_recv()
+    up_a2 = hop(near.at[first], far.at[first], 2, above)
+    up_a2.start()
+    down_b.wait_recv()
+    down_b2 = hop(near.at[fourth], far.at[second], 3, below)
+    down_b2.start()
+    up_b = hop(normed_ref.at[second], near.at[second], 4, above)
+    down_a = hop(normed_ref.at[first], near.at[third], 5, below)
+    up_b.start()
+    down_a.start()
+    own_out[...] = hidden_units(normed_ref[...])
+    finals.finish_core()
+    finals.start_z()
+    up_a2.wait_recv()
+    down_b2.wait_recv()
+    far_out[...] = hidden_units(far[...]).astype(jnp.bfloat16)
+    far_up = hop(far_out.at[first], far_in.at[first], 6, above)
+    far_down = hop(far_out.at[second], far_in.at[second], 7, below)
+    far_up.start()
+    far_down.start()
+    finals.finish_z()
+    finals.start_x()
+    up_b.wait_recv()
+    down_a.wait_recv()
+    near_out[...] = hidden_units(near[...]).astype(jnp.bfloat16)
+    back_down = hop(near_out.at[first], high_in.at[first], 8, below)
+    back_up = hop(near_out.at[fourth], low_in.at[second], 9, above)
+    back_down.start()
+    back_up.start()
+    finals.finish_x()
+    finals.start_z2()
+
+    def joined(rows_at, extra):
+        return (
+            near_out[rows_at].astype(jnp.float32) + far_in[extra].astype(jnp.float32)
+        ).astype(jnp.bfloat16)
+
+    far_up.wait_recv()
+    near_out[third] = joined(third, first)
+    last_up = hop(near_out.at[third], low_in.at[first], 10, above)
+    last_up.start()
+    far_down.wait_recv()
+    near_out[second] = joined(second, second)
+    last_down = hop(near_out.at[second], high_in.at[second], 11, below)
+    last_down.start()
+    finals.finish_z2()
+    finals.start_core2()
+    finals.finish_core2(full)
+    state = jnp.zeros((STATE, inner), jnp.float32)
+    edge = jnp.zeros((16, inner), jnp.float32)
+    for r in range(requests):
+        owned = info[12 + r] == me
+        state = jnp.where(owned, full[2 * r].astype(jnp.float32), state)
+        edge = jnp.where(owned, full[2 * r + 1].astype(jnp.float32), edge)
+    new_state_ref[...] = state
+    new_edge_ref[...] = edge[:EDGE].astype(jnp.bfloat16)
+    own_out[...] = own_out[...] + middle_ref[...]
+    back_down.wait_recv()
+    back_up.wait_recv()
+    last_up.wait_recv()
+    last_down.wait_recv()
+    total = own_out[...] + low_in[...].astype(jnp.float32) + high_in[...].astype(jnp.float32)
+    out_ref[...] = jnp.transpose(total).astype(jnp.bfloat16)
+    for copy in (
+        up_a, down_b, up_a2, down_b2, up_b, down_a,
+        far_up, far_down, back_down, back_up, last_up, last_down,
+    ):
+        copy.wait_send()
+
+
+def mlp_call(devices, info, args, weights, rows, model, inner, requests):
+    f32, bf16 = jnp.float32, jnp.bfloat16
+    hidden = weights[0].shape[1]
+    return pl.pallas_call(
+        functools.partial(mlp_stage, devices),
+        out_shape=(
+            jax.ShapeDtypeStruct((model, rows), bf16),
+            jax.ShapeDtypeStruct((STATE, inner), f32),
+            jax.ShapeDtypeStruct((EDGE, inner), bf16),
+        ),
+        in_specs=[sspec()]
+        + [vspec()] * len(args)
+        + [pl.BlockSpec(memory_space=pl.ANY)] * len(weights),
+        out_specs=tuple([vspec()] * 3),
+        scratch_shapes=[
+            VMEM((model, hidden), bf16),
+            VMEM((model, hidden), bf16),
+            VMEM((model, hidden), bf16),
+            pltpu.SemaphoreType.DMA((3,)),
+            VMEM((2 * rows, model), bf16),
+            VMEM((rows, model), bf16),
+            VMEM((2 * rows, model), bf16),
+            VMEM((rows, model), bf16),
+            VMEM((rows, model), f32),
+            VMEM((rows, model), bf16),
+            VMEM((rows, model), bf16),
+            VMEM((rows, model), bf16),
+            pltpu.SemaphoreType.DMA((2, 12)),
+            VMEM((2 * requests, 16, inner), bf16),
+        ]
+        + Spread.scratch(devices, inner, 2 * requests, True),
+        compiler_params=pltpu.CompilerParams(
+            vmem_limit_bytes=56 << 20, collective_id=1, has_side_effects=True
+        ),
+        cost_estimate=pl.CostEstimate(
+            flops=7_000_000_000, bytes_accessed=16_000_000, transcendentals=1_000_000
+        ),
+        name="mlp_stage",
+    )(info, *args, *weights)
 
 
 def shards(
@@ -414,28 +949,16 @@
             jnp.reshape(place * rows, (1,)).astype(jnp.int32),
         ]
     )
-    bf16 = jnp.bfloat16
-    states = lax.all_gather(cache_state[0, 0].astype(bf16), "seq")
-    edges = lax.all_gather(cache_edge[0, 0], "seq")
-    chooser = (
-        cont_flag[0][:, None]
-        * (cache_source[0][:, None] == jnp.arange(devices)[None, :]).astype(jnp.int32)
-    ).astype(jnp.float32)
-    start_state = picked(states.astype(jnp.float32), chooser)
-    start_edge = picked(edges.astype(jnp.float32), chooser).astype(bf16)
-    start_edge = start_edge.reshape(requests * EDGE, inner)
-    start_edge = jnp.pad(start_edge, ((0, 16 - requests * EDGE), (0, 0)))
-    halo = passed_along(mamba_in[0, rows - 16 :], "seq", 1)
-    mixed, step, proj, end_state, step_sum, last_edge = token_call(
+    mixed, step, proj, enter, last_edge, start_state = front_call(
+        devices,
         info,
         (
             mamba_in[0],
-            halo,
-            start_edge,
-            start_state,
+            cache_state[0, 0],
+            cache_edge[0, 0],
             conv_weight,
             conv_bias[None],
-            x_proj,
+            x_proj.T,
             dt_proj,
             dt_bias[None],
             decay_rate[None],
@@ -443,17 +966,8 @@
         rows,
         inner,
         x_proj.shape[1],
+        requests,
     )
-    all_end = lax.all_gather(end_state, "seq")
-    all_sum = lax.all_gather(step_sum[0], "seq")
-    rates = (jnp.arange(STATE) + 1).astype(jnp.float32)[:, None] * decay_rate[None, :]
-    enter = jnp.zeros_like(end_state)
-
-    def lap(k, before):
-        after = jnp.exp(-rates * all_sum[k][None]) * before + all_end[k]
-        return jnp.where(k < place, after, before)
-
-    enter = lax.fori_loop(0, devices, lap, enter)
     middle, normed, finals = scan_call(
         info,
         (
@@ -464,37 +978,26 @@
             start_state,
             decay_rate[None],
             skip_gain[None],
-            hidden_in[0],
+            hidden_in[0].T,
             norm_gain[None],
         ),
-        out_proj,
+        out_proj.T,
         rows,
         inner,
         model,
         requests,
     )
-    sums = jnp.concatenate([finals.reshape(requests * STATE, inner), last_edge], axis=0)
-    sums = lax.psum(sums.astype(bf16), "seq")
-    owned = (owner_slot[0] == place).astype(bf16)
-    new_state = jnp.einsum("r,rsc->sc", owned, sums[: requests * STATE].reshape(finals.shape))
-    last = sums[requests * STATE :][: requests * EDGE].reshape(requests, EDGE, inner)
-    new_edge = jnp.einsum("r,rsc->sc", owned, last)
-    piece = lax.all_gather(normed, "req", axis=0, tiled=True)
-    gate_v = jnp.dot(piece, mlp_gate, preferred_element_type=jnp.float32)
-    up_v = jnp.dot(piece, mlp_up, preferred_element_type=jnp.float32)
-    hidden = (jax.nn.silu(gate_v) * up_v).astype(bf16)
-    mlp_out = lax.psum_scatter(
-        jnp.dot(hidden, mlp_down, preferred_element_type=jnp.float32).astype(bf16),
-        "req",
-        scatter_dimension=0,
-        tiled=True,
-    ).astype(jnp.float32)
-    block_rows = (middle + mlp_out).astype(bf16)
-    return (
-        block_rows[None],
-        new_state.astype(jnp.float32)[None, None],
-        new_edge.astype(bf16)[None, None],
+    block_out, new_state, new_edge = mlp_call(
+        devices,
+        info,
+        (normed, middle, finals, last_edge),
+        (mlp_gate, mlp_up, mlp_down.T),
+        rows,
+        model,
+        inner,
+        requests,
     )
+    return block_out.T[None], new_state[None, None], new_edge[None, None]
 
 
 def solution(mesh):

time: 387 us -> 125 us (0.32)
  waiting for transfers between devices: 158 us -> 0 us
  Pallas kernels: 26.1 us -> 103 us
  blocking collectives: 51.4 us -> 0 us
  local copies, waits for them, and re-layouts: 68.4 us -> 19.3 us
  other arithmetic: 40.2 us -> 0 us
  matrix products: 22.8 us -> 0 us
  between operations: 14.1 us -> 0.72 us
    psum x1 -> x0, waiting for transfers between devices: 87.1 us -> none  [shards(): sums = lax.psum(sums.astype(bf16), 'seq')]
    pallas_call x1 -> x2, Pallas kernels: 9.29 us -> 85.6 us  [the longest x1 46.2 us: front_call(): pl.pallas_call(functools.partial(front_stage, devices), out_shape=(jax.Sh...]
    all_gather x2 -> x0, blocking collectives: 51.4 us -> none  [the longest x1 26.9 us: shards(): edges = lax.all_gather(cache_edge[0, 0], 'seq')]
    all_gather x3 -> x0, waiting for transfers between devices: 46 us -> none  [the longest x1 24.7 us: shards(): piece = lax.all_gather(normed, 'req', axis=0, tiled=True)]
    select_n x32 -> x0, other arithmetic: 34.8 us -> none  [lap(): return jnp.where(k < place, after, before)]
    dynamic_slice x32 -> x0, local copies, waits for them, and re-layouts: 30.1 us -> none  [lap(): after = jnp.exp(-rates * all_sum[k][None]) * before + all_end[k]]
    reduce_scatter x1 -> x0, waiting for transfers between devices: 24.6 us -> none  [shards(): lax.psum_scatter(jnp.dot(hidden, mlp_down, preferred_element_type=jnp.flo...]
    dot_general x6 -> x0, matrix products: 22.8 us -> none  [the longest x1 10.1 us: shards(): jnp.dot(hidden, mlp_down, preferred_element_type=jnp.float32).astype(bf16)]
  transfers between devices with their start and end apart: 6 -> 0, of which waited for: 5 -> 0; matrix products, arithmetic and copies ran while one was open for 14% -> 0% of each run, Pallas kernels for 0% -> 0%
where the time goes in v1:
time: 125 us; the launch traced here: 123 us
  Pallas kernels  103 us (82%)
  local copies, waits for them, and re-layouts  19.3 us (15%)
    pallas_call x1, Pallas kernels, front_call(): pl.pallas_call(functools.partial(front_stage, devices), out_shape=(jax.Sh...  46.2 us
    pallas_call x1, Pallas kernels, mlp_call(): pl.pallas_call(functools.partial(mlp_stage, devices), out_shape=(jax.Shap...  39.4 us
    pallas_call x1, Pallas kernels, scan_call(): pl.pallas_call(scan_stage, out_shape=(jax.ShapeDtypeStruct((rows, model),...  17.4 us
    unnamed x27, local copies, waits for them, and re-layouts  14.9 us

profile of v1, /device:TPU:0, one launch (start us, length us, event | category | flops | bytes accessed | tf_op | source)
XLA Modules:
  0.0 123.1 jit_solution(12462593002056974920)
XLA Ops:
  0.6 0.8 concatenate.3.info
  1.4 0.0 copy-start.1
  1.4 0.7 broadcast_in_dim.29.gain_ref
  2.1 0.7 broadcast_in_dim.27.decay_ref
  2.9 0.7 broadcast_in_dim.25.conv_b_ref
  3.6 0.7 broadcast_in_dim.26.dt_bias_ref
  4.3 0.7 broadcast_in_dim.28.skip_ref
  5.0 0.0 copy-start.2
  5.1 1.2 copy-done.2
  6.2 0.0 copy-start.4
  6.2 1.1 copy-done.4
  7.4 0.0 copy-start.6
  7.4 1.1 copy-done.6
  8.5 0.0 copy-start.8
  8.5 0.9 copy-done.8
  9.4 0.0 copy-start.9
  9.4 0.8 copy-done.9
  10.2 0.0 copy-start.10
  10.2 0.7 copy-done.10
  10.9 46.2 %front_stage.1 = (f32[128,3200]{1,0:T(8,128)S(1)}, f32[128,3200]{1,0:T(8,128)}, f32[128,132]{1,0:T(8,128)S(1)}, f32[16,3200]{1,0:T(8,128)S(1)}, f32[16,3200]{1,0...) custom-call(s32[17]{0:T(128)S(1)} %concatenate.3.info, bf16[128,3200]{1,0:T(8,128)(2,1)S(1)} %bitcast.21, ...), custom_call_target="tpu_custom_call" | custom-call | flops 400000000 | bytes 8000000 | tf_op jit(solution)/shard_map/front_stage/pallas_call | solution.py:522
  57.1 0.0 copy-start.11
  57.1 0.7 copy-done.11
  57.8 0.0 copy-start
  57.8 1.0 copy-done
  58.8 17.4 %scan_stage.1 = (f32[128,1600]{1,0:T(8,128)S(1)}, bf16[128,1600]{1,0:T(8,128)(2,1)S(1)}, f32[4,16,3200]{2,1,0:T(8,128)S(1)}) custom-call(s32[17]{0:T(128)S(1)} %concatenate.3.info, f32[128,3200]{1,0:T(8,128)S(1)} %get-tuple-element.15.mixed_ref, f32[128,3200]{1,0:T(8,128)} %get-tuple-element.16.step_ref, f32[128,132]{1,0:T(8,128)S(1)} %get-tuple-element.17.proj_ref, ...), custom_call_target="tpu_custom_call" | custom-call | flops 1400000000 | bytes 18000000 | tf_op jit(solution)/shard_map/scan_stage/pallas_call | solution.py:699
  76.3 0.0 copy-done.1
  76.3 0.0 copy-start.3
  76.3 0.9 copy-done.3
  77.2 0.0 copy-start.5
  77.2 0.9 copy-done.5
  78.1 0.0 copy-start.7
  78.1 0.8 copy-done.7
  78.9 39.4 %mlp_stage.1 = (bf16[1600,128]{1,0:T(8,128)(2,1)}, f32[16,3200]{1,0:T(8,128)}, bf16[3,3200]{1,0:T(4,128)(2,1)}) custom-call(s32[17]{0:T(128)} %copy-done.1, bf16[128,1600]{1,0:T(8,128)(2,1)} %copy-done.7, f32[128,1600]{1,0:T(8,128)} %copy-done.3, f32[4,16,3200]{2,1,0:T(8,128)} %copy-done.5, f32[16,3200]{1,0:T(8,128)} %copy-done.11, ...), custom_call_target="tpu_custom_call" | custom-call | flops 7000000000 | bytes 16000000 | tf_op jit(solution)/shard_map/mlp_stage/pallas_call | solution.py:878
  118.3 1.8 %copy.26 = bf16[1,128,1600]{1,2,0:T(8,128)(2,1)} copy(bf16[1,128,1600]{1,2,0:T(8,128)(2,1)} %bitcast.25) | data formatting | bytes 819200
  120.1 1.6 %copy.27 = f32[1,1,16,3200]{3,2,1,0:T(8,128)} copy(f32[1,1,16,3200]{3,2,1,0:T(8,128)} %bitcast.26) | data formatting | bytes 409600
  121.7 1.4 %copy.28 = bf16[1,1,3,3200]{3,2,1,0:T(4,128)(2,1)} copy(bf16[1,1,3,3200]{3,2,1,0:T(4,128)(2,1)} %bitcast.27) | data formatting | bytes 38400
Async XLA Ops:
  1.4 74.8 %copy-start.1 = (s32[17]{0:T(128)}, s32[17]{0:T(128)S(1)}, u32[]{:S(2)}) copy-start(s32[17]{0:T(128)S(1)} %concatenate.3.info) | copy-start | bytes 208
  5.0 1.2 copy-start.2
  6.2 1.1 copy-start.4
  7.4 1.1 copy-start.6
  8.5 0.9 copy-start.8
  9.4 0.8 copy-start.9
  10.2 0.7 copy-start.10
  57.1 0.7 copy-start.11
  57.8 1.0 copy-start
  76.3 0.9 copy-start.3
  77.2 0.9 copy-start.5
  78.1 0.8 copy-start.7

commit v2 on v1

--- a/solution.py
+++ b/solution.py
@@ -19,6 +19,10 @@
 
 def vspec():
     return pl.BlockSpec(memory_space=VMEM)
+
+
+def hspec():
+    return pl.BlockSpec(memory_space=pltpu.HBM)
 
 
 def sspec():
@@ -216,21 +220,30 @@
 def front_stage(
     devices,
     info,
-    x_ref,
-    cache_ref,
-    cache_edge_ref,
-    conv_w_ref,
-    conv_b_ref,
-    x_proj_ref,
-    dt_proj_ref,
-    dt_bias_ref,
-    decay_ref,
+    taps_ref,
+    conv_b_flat,
+    dt_bias_flat,
+    decay_flat,
+    skip_flat,
+    gain_flat,
+    x_hbm,
+    cache_hbm,
+    cache_edge_hbm,
+    x_proj_hbm,
+    dt_proj_hbm,
     mixed_ref,
     step_ref,
     proj_ref,
     enter_ref,
     last_edge_ref,
     start_ref,
+    param_ref,
+    x_ref,
+    cache_ref,
+    cache_edge_ref,
+    x_proj_ref,
+    dt_proj_ref,
+    fetch_sems,
     ext,
     mixed_b,
     suffix,
@@ -253,13 +266,37 @@
     pre_sems,
     *spread_refs,
 ):
+    fetches = [
+        pltpu.make_async_copy(src, dst, fetch_sems.at[i])
+        for i, (src, dst) in enumerate(
+            (
+                (x_hbm, x_ref),
+                (cache_edge_hbm, cache_edge_ref),
+                (cache_hbm, cache_ref),
+                (x_proj_hbm, x_proj_ref),
+                (dt_proj_hbm, dt_proj_ref),
+            )
+        )
+    ]
+    for copy in fetches:
+        copy.start()
+    param_ref[pl.ds(0, 4), :] = taps_ref[...]
+    for i, flat in enumerate((conv_b_flat, dt_bias_flat, decay_flat, skip_flat, gain_flat)):
+        size = flat.shape[0]
+        param_ref[pl.ds(4 + i, 1), pl.ds(0, size)] = flat[...].reshape(1, size)
+    conv_w_ref = param_ref.at[pl.ds(0, 4)]
+    conv_b_ref = param_ref.at[pl.ds(4, 1)]
+    dt_bias_ref = param_ref.at[pl.ds(5, 1)]
+    decay_ref = param_ref.at[pl.ds(6, 1)]
     rows, inner = x_ref.shape
     requests = start_ref.shape[0]
     me, core, z, x, partner, z_peers, x_peers = near_devices(devices)
     after, before = (me + 1) % devices, (me + devices - 1) % devices
     greet([("seq", p) for p in [partner, after, before] + z_peers + x_peers])
     halo_copy = send(x_ref.at[pl.ds(rows - 16, 16)], halo_ref, halo_sems, 0, after)
+    fetches[0].wait()
     halo_copy.start()
+    fetches[1].wait()
     per = len(Spread.scratch(devices, inner, 1, False))
     edge_sum = Spread(devices, inner, 1, False, spread_refs[:per])
     state_sum = Spread(devices, inner, requests, True, spread_refs[per:])
@@ -272,11 +309,14 @@
             placed = jnp.where((spot == r * EDGE + j) & take, edge_rows[j : j + 1], placed)
     edge_sum.mine[0] = placed.astype(jnp.bfloat16)
     edge_sum.start_core()
+    fetches[2].wait()
     for r in range(requests):
         take = (info[8 + r] == me) & (info[4 + r] > 0)
         state_sum.mine[r] = jnp.where(take, cache_ref[...], 0.0).astype(jnp.bfloat16)
     state_sum.start_core()
     ext[pl.ds(16, rows), :] = x_ref[...].astype(jnp.float32)
+    fetches[3].wait()
+    fetches[4].wait()
     edge_sum.finish_core()
     edge_sum.start_z()
     state_sum.finish_core()
@@ -528,10 +568,17 @@
             jax.ShapeDtypeStruct((STATE, inner), f32),
             jax.ShapeDtypeStruct((16, inner), f32),
             jax.ShapeDtypeStruct((requests, STATE, inner), bf16),
+            jax.ShapeDtypeStruct((16, inner), f32),
         ),
-        in_specs=[sspec()] + [vspec()] * len(args),
-        out_specs=tuple([vspec()] * 6),
+        in_specs=[sspec()] + [vspec()] * 6 + [hspec()] * (len(args) - 6),
+        out_specs=tuple([vspec()] * 7),
         scratch_shapes=[
+            VMEM((rows, inner), bf16),
+            VMEM((STATE, inner), f32),
+            VMEM((EDGE, inner), bf16),
+            VMEM((proj_width, inner), bf16),
+            VMEM((proj_width - 2 * STATE, inner), bf16),
+            pltpu.SemaphoreType.DMA((5,)),
             VMEM((rows + 16, inner), f32),
             VMEM((rows, inner), bf16),
             VMEM((rows, inner), f32),
@@ -556,7 +603,7 @@
         + Spread.scratch(devices, inner, 1, False)
         + Spread.scratch(devices, inner, requests, True),
         compiler_params=pltpu.CompilerParams(
-            vmem_limit_bytes=48 << 20, collective_id=0, has_side_effects=True
+            vmem_limit_bytes=61 << 20, collective_id=0, has_side_effects=True
         ),
         cost_estimate=pl.CostEstimate(
             flops=400_000_000, bytes_accessed=8_000_000, transcendentals=2_000_000
@@ -572,10 +619,8 @@
     proj_ref,
     enter_ref,
     start_ref,
-    decay_ref,
-    skip_ref,
-    hidden_ref,
-    gain_ref,
+    param_ref,
+    hidden_hbm,
     out_w_hbm,
     middle_ref,
     normed_ref,
@@ -584,7 +629,9 @@
     y_ref,
     ssm_b,
     out_w,
+    hidden_ref,
     w_sem,
+    hidden_sem,
 ):
     rows, inner = mixed_ref.shape
     width = col_block(inner)
@@ -592,6 +639,11 @@
     rank = proj_ref.shape[1] - 2 * STATE
     fetch = pltpu.make_async_copy(out_w_hbm, out_w, w_sem)
     fetch.start()
+    fetch_hidden = pltpu.make_async_copy(hidden_hbm, hidden_ref, hidden_sem)
+    fetch_hidden.start()
+    model = hidden_ref.shape[0]
+    decay_ref = param_ref.at[pl.ds(6, 1)]
+    skip_ref = param_ref.at[pl.ds(7, 1)]
 
     turned = jnp.transpose(proj_ref[:, rank : rank + 2 * STATE])
     for t in range(rows):
@@ -681,6 +733,7 @@
 
     lax.fori_loop(0, inner // width, one_block, 0)
     fetch.wait()
+    fetch_hidden.wait()
     middle = jnp.transpose(hidden_ref[...].astype(jnp.float32))
     for first in range(0, inner, width):
         middle = middle + lax.dot_general(
@@ -691,7 +744,7 @@
         )
     middle_ref[...] = middle
     scale = lax.rsqrt(jnp.mean(middle * middle, axis=1, keepdims=True) + NORM_EPS)
-    normed_ref[...] = (middle * scale * gain_ref[...]).astype(jnp.bfloat16)
+    normed_ref[...] = (middle * scale * param_ref[8:9, :model]).astype(jnp.bfloat16)
 
 
 def scan_call(info, args, out_w, rows, inner, model, requests):
@@ -703,16 +756,18 @@
             jax.ShapeDtypeStruct((rows, model), jnp.bfloat16),
             jax.ShapeDtypeStruct((requests, STATE, inner), f32),
         ),
-        in_specs=[sspec()] + [vspec()] * len(args) + [pl.BlockSpec(memory_space=pl.ANY)],
+        in_specs=[sspec()] + [vspec()] * (len(args) - 1) + [hspec()] * 2,
         out_specs=tuple([vspec()] * 3),
         scratch_shapes=[
             VMEM((rows, 2 * STATE, LANES), f32),
             VMEM((rows, inner), f32),
             VMEM((rows, inner), jnp.bfloat16),
             VMEM((model, inner), jnp.bfloat16),
+            VMEM((model, rows), jnp.bfloat16),
+            pltpu.SemaphoreType.DMA,
             pltpu.SemaphoreType.DMA,
         ],
-        compiler_params=pltpu.CompilerParams(vmem_limit_bytes=48 << 20),
+        compiler_params=pltpu.CompilerParams(vmem_limit_bytes=61 << 20),
         cost_estimate=pl.CostEstimate(
             flops=1_400_000_000, bytes_accessed=18_000_000, transcendentals=4_000_000
         ),
@@ -723,23 +778,29 @@
 def mlp_stage(
     devices,
     info,
-    normed_ref,
-    middle_ref,
-    final_ref,
-    last_edge_ref,
+    normed_hbm,
+    middle_hbm,
+    final_hbm,
+    last_edge_hbm,
     gate_hbm,
     up_hbm,
     down_hbm,
     out_ref,
     new_state_ref,
     new_edge_ref,
+    normed_ref,
+    middle_ref,
+    final_ref,
+    last_edge_ref,
     gate_w,
     up_w,
     down_w,
-    w_sems,
-    near,
+    fetch_sems,
+    near1,
+    near2,
     far,
-    near_out,
+    out1,
+    out2,
     far_out,
     own_out,
     low_in,
@@ -747,6 +808,7 @@
     far_in,
     ring_sems,
     full,
+    full_edge,
     *spread_refs,
 ):
     rows, model = normed_ref.shape
@@ -758,9 +820,18 @@
     here = lax.axis_index("req")
     above, below = (here + 1) % ring, (here + ring - 1) % ring
     fetches = [
-        pltpu.make_async_copy(gate_hbm, gate_w, w_sems.at[0]),
-        pltpu.make_async_copy(up_hbm, up_w, w_sems.at[1]),
-        pltpu.make_async_copy(down_hbm, down_w, w_sems.at[2]),
+        pltpu.make_async_copy(src, dst, fetch_sems.at[i])
+        for i, (src, dst) in enumerate(
+            (
+                (normed_hbm, normed_ref),
+                (final_hbm, final_ref),
+                (last_edge_hbm, last_edge_ref),
+                (gate_hbm, gate_w),
+                (up_hbm, up_w),
+                (down_hbm, down_w),
+                (middle_hbm, middle_ref),
+            )
+        )
     ]
     for copy in fetches:
         copy.start()
@@ -779,18 +850,31 @@
         )
 
     first, second = pl.ds(0, half), pl.ds(half, half)
-    third, fourth = pl.ds(2 * half, half), pl.ds(3 * half, half)
-    up_a = hop(normed_ref.at[first], near.at[first], 0, above)
-    down_b = hop(normed_ref.at[second], near.at[fourth], 1, below)
+    up_a = hop(normed_ref.at[first], near1.at[first], 0, above)
+    down_b = hop(normed_ref.at[second], near1.at[second], 1, below)
+    up_a2 = hop(near1.at[first], far.at[first], 2, above)
+    down_b2 = hop(near1.at[second], far.at[second], 3, below)
+    up_b = hop(normed_ref.at[second], near2.at[first], 4, above)
+    down_a = hop(normed_ref.at[first], near2.at[second], 5, below)
+    far_up = hop(far_out.at[first], far_in.at[first], 6, above)
+    far_down = hop(far_out.at[second], far_in.at[second], 7, below)
+    back_down = hop(out1.at[first], high_in.at[first], 8, below)
+    back_up = hop(out1.at[second], low_in.at[second], 9, above)
+    last_down = hop(out2.at[first], high_in.at[second], 10, below)
+    last_up = hop(out2.at[second], low_in.at[first], 11, above)
+    fetches[0].wait()
     up_a.start()
     down_b.start()
-    finals = Spread(devices, inner, requests + requests, True, spread_refs)
+    per = len(Spread.scratch(devices, inner, 1, False))
+    finals = Spread(devices, inner, requests, True, spread_refs[:per])
+    edges = Spread(devices, inner, 1, False, spread_refs[per:])
+    fetches[1].wait()
     for r in range(requests):
-        finals.mine[2 * r] = final_ref[r].astype(jnp.bfloat16)
-        edges = last_edge_ref[pl.ds(r * EDGE, EDGE), :]
-        rest = jnp.zeros((16 - EDGE, inner), jnp.float32)
-        finals.mine[2 * r + 1] = jnp.concatenate([edges, rest], axis=0).astype(jnp.bfloat16)
+        finals.mine[r] = final_ref[r].astype(jnp.bfloat16)
     finals.start_core()
+    fetches[2].wait()
+    edges.mine[0] = last_edge_ref[...].astype(jnp.bfloat16)
+    edges.start_core()
 
     def hidden_units(value):
         gate = jnp.dot(value, gate_w[...], preferred_element_type=jnp.float32)
@@ -800,65 +884,58 @@
             hidden, down_w[...], (((1,), (1,)), ((), ())), preferred_element_type=jnp.float32
         )
 
-    for copy in fetches:
+    finals.finish_core()
+    finals.start_z()
+    edges.finish_core()
+    for copy in fetches[3:]:
         copy.wait()
     up_a.wait_recv()
-    up_a2 = hop(near.at[first], far.at[first], 2, above)
     up_a2.start()
     down_b.wait_recv()
-    down_b2 = hop(near.at[fourth], far.at[second], 3, below)
     down_b2.start()
-    up_b = hop(normed_ref.at[second], near.at[second], 4, above)
-    down_a = hop(normed_ref.at[first], near.at[third], 5, below)
     up_b.start()
     down_a.start()
-    own_out[...] = hidden_units(normed_ref[...])
-    finals.finish_core()
-    finals.start_z()
+    out1[...] = hidden_units(near1[...]).astype(jnp.bfloat16)
+    finals.finish_z()
+    finals.start_x()
+    edges.start_z()
     up_a2.wait_recv()
     down_b2.wait_recv()
     far_out[...] = hidden_units(far[...]).astype(jnp.bfloat16)
-    far_up = hop(far_out.at[first], far_in.at[first], 6, above)
-    far_down = hop(far_out.at[second], far_in.at[second], 7, below)
     far_up.start()
     far_down.start()
-    finals.finish_z()
-    finals.start_x()
+    back_down.start()
+    back_up.start()
     up_b.wait_recv()
     down_a.wait_recv()
-    near_out[...] = hidden_units(near[...]).astype(jnp.bfloat16)
-    back_down = hop(near_out.at[first], high_in.at[first], 8, below)
-    back_up = hop(near_out.at[fourth], low_in.at[second], 9, above)
-    back_down.start()
-    back_up.start()
+    own_out[...] = hidden_units(near2[...])
     finals.finish_x()
     finals.start_z2()
-
-    def joined(rows_at, extra):
-        return (
-            near_out[rows_at].astype(jnp.float32) + far_in[extra].astype(jnp.float32)
-        ).astype(jnp.bfloat16)
-
+    far_down.wait_recv()
+    out2[first] = (own_out[first] + far_in[second].astype(jnp.float32)).astype(jnp.bfloat16)
+    last_down.start()
     far_up.wait_recv()
-    near_out[third] = joined(third, first)
-    last_up = hop(near_out.at[third], low_in.at[first], 10, above)
+    out2[second] = (own_out[second] + far_in[first].astype(jnp.float32)).astype(jnp.bfloat16)
     last_up.start()
-    far_down.wait_recv()
-    near_out[second] = joined(second, second)
-    last_down = hop(near_out.at[second], high_in.at[second], 11, below)
-    last_down.start()
+    edges.finish_z()
+    edges.start_x()
+    own_out[...] = hidden_units(normed_ref[...]) + middle_ref[...]
     finals.finish_z2()
     finals.start_core2()
+    edges.finish_x()
+    edges.start_core2()
     finals.finish_core2(full)
     state = jnp.zeros((STATE, inner), jnp.float32)
-    edge = jnp.zeros((16, inner), jnp.float32)
+    for r in range(requests):
+        state = jnp.where(info[12 + r] == me, full[r].astype(jnp.float32), state)
+    new_state_ref[...] = state
+    edges.finish_core2(full_edge)
+    gathered = full_edge[0].astype(jnp.float32)
+    edge = jnp.zeros((EDGE, inner), jnp.float32)
     for r in range(requests):
         owned = info[12 + r] == me
-        state = jnp.where(owned, full[2 * r].astype(jnp.float32), state)
-        edge = jnp.where(owned, full[2 * r + 1].astype(jnp.float32), edge)
-    new_state_ref[...] = state
-    new_edge_ref[...] = edge[:EDGE].astype(jnp.bfloat16)
-    own_out[...] = own_out[...] + middle_ref[...]
+        edge = jnp.where(owned, gathered[r * EDGE : (r + 1) * EDGE], edge)
+    new_edge_ref[...] = edge.astype(jnp.bfloat16)
     back_down.wait_recv()
     back_up.wait_recv()
     last_up.wait_recv()
@@ -882,35 +959,64 @@
             jax.ShapeDtypeStruct((STATE, inner), f32),
             jax.ShapeDtypeStruct((EDGE, inner), bf16),
         ),
-        in_specs=[sspec()]
-        + [vspec()] * len(args)
-        + [pl.BlockSpec(memory_space=pl.ANY)] * len(weights),
+        in_specs=[sspec()] + [hspec()] * (len(args) + len(weights)),
         out_specs=tuple([vspec()] * 3),
         scratch_shapes=[
+            VMEM((rows, model), bf16),
+            VMEM((rows, model), f32),
+            VMEM((requests, STATE, inner), f32),
+            VMEM((16, inner), f32),
             VMEM((model, hidden), bf16),
             VMEM((model, hidden), bf16),
             VMEM((model, hidden), bf16),
-            pltpu.SemaphoreType.DMA((3,)),
-            VMEM((2 * rows, model), bf16),
+            pltpu.SemaphoreType.DMA((7,)),
             VMEM((rows, model), bf16),
-            VMEM((2 * rows, model), bf16),
+            VMEM((rows, model), bf16),
+            VMEM((rows, model), bf16),
+            VMEM((rows, model), bf16),
+            VMEM((rows, model), bf16),
             VMEM((rows, model), bf16),
             VMEM((rows, model), f32),
             VMEM((rows, model), bf16),
             VMEM((rows, model), bf16),
             VMEM((rows, model), bf16),
             pltpu.SemaphoreType.DMA((2, 12)),
-            VMEM((2 * requests, 16, inner), bf16),
+            VMEM((requests, 16, inner), bf16),
+            VMEM((1, 16, inner), bf16),
         ]
-        + Spread.scratch(devices, inner, 2 * requests, True),
+        + Spread.scratch(devices, inner, requests, True)
+        + Spread.scratch(devices, inner, 1, False),
         compiler_params=pltpu.CompilerParams(
-            vmem_limit_bytes=56 << 20, collective_id=1, has_side_effects=True
+            vmem_limit_bytes=61 << 20, collective_id=1, has_side_effects=True
         ),
         cost_estimate=pl.CostEstimate(
             flops=7_000_000_000, bytes_accessed=16_000_000, transcendentals=1_000_000
         ),
         name="mlp_stage",
     )(info, *args, *weights)
+
+
+def handing_stage(*refs):
+    count = (len(refs) - 1) // 2
+    sems = refs[-1]
+    copies = [
+        pltpu.make_async_copy(refs[i], refs[count + i], sems.at[i]) for i in range(count)
+    ]
+    for copy in copies:
+        copy.start()
+    for copy in copies:
+        copy.wait()
+
+
+def handed(*arrays):
+    return pl.pallas_call(
+        handing_stage,
+        out_shape=tuple(jax.ShapeDtypeStruct(a.shape, a.dtype) for a in arrays),
+        in_specs=[pl.BlockSpec(memory_space=pl.ANY)] * len(arrays),
+        out_specs=tuple([hspec()] * len(arrays)),
+        scratch_shapes=[pltpu.SemaphoreType.DMA((len(arrays),))],
+        name="handing_stage",
+    )(*arrays)
 
 
 def shards(
@@ -949,19 +1055,21 @@
             jnp.reshape(place * rows, (1,)).astype(jnp.int32),
         ]
     )
-    mixed, step, proj, enter, last_edge, start_state = front_call(
+    mixed, step, proj, enter, last_edge, start_state, params = front_call(
         devices,
         info,
         (
+            conv_weight,
+            conv_bias,
+            dt_bias,
+            decay_rate,
+            skip_gain,
+            norm_gain,
             mamba_in[0],
             cache_state[0, 0],
             cache_edge[0, 0],
-            conv_weight,
-            conv_bias[None],
             x_proj.T,
             dt_proj,
-            dt_bias[None],
-            decay_rate[None],
         ),
         rows,
         inner,
@@ -970,32 +1078,24 @@
     )
     middle, normed, finals = scan_call(
         info,
-        (
-            mixed,
-            step,
-            proj,
-            enter,
-            start_state,
-            decay_rate[None],
-            skip_gain[None],
-            hidden_in[0].T,
-            norm_gain[None],
-        ),
+        (mixed, step, proj, enter, start_state, params, hidden_in[0].T),
         out_proj.T,
         rows,
         inner,
         model,
         requests,
     )
-    block_out, new_state, new_edge = mlp_call(
-        devices,
-        info,
-        (normed, middle, finals, last_edge),
-        (mlp_gate, mlp_up, mlp_down.T),
-        rows,
-        model,
-        inner,
-        requests,
+    block_out, new_state, new_edge = handed(
+        *mlp_call(
+            devices,
+            info,
+            (normed, middle, finals, last_edge),
+            (mlp_gate, mlp_up, mlp_down.T),
+            rows,
+            model,
+            inner,
+            requests,
+        )
     )
     return block_out.T[None], new_state[None, None], new_edge[None, None]
 

time: 125 us -> 128 us (1.024); the launches traced: 123 us -> 128 us
  Pallas kernels: 103 us -> 125 us
  local copies, waits for them, and re-layouts: 19.3 us -> 1.3 us
    pallas_call x0 -> x1, Pallas kernels: none -> 20.5 us  [handed(): pl.pallas_call(handing_stage, out_shape=tuple((jax.ShapeDtypeStruct(a.sha...]
    unnamed x27 -> x0, local copies, waits for them, and re-layouts: 14.9 us -> none
    broadcast_in_dim x5 -> x0, local copies, waits for them, and re-layouts: 3.62 us -> none  [the longest x1 0.73 us: shards(): dt_bias[None]]
    pallas_call x1, Pallas kernels: 17.4 us -> 19.4 us  [scan_call(): pl.pallas_call(scan_stage, out_shape=(jax.ShapeDtypeStruct((rows, model),...]
where the time goes in v2:
time: 128 us
  Pallas kernels  125 us (98%)
  local copies, waits for them, and re-layouts  1.3 us (1%)
    pallas_call x1, Pallas kernels, front_call(): pl.pallas_call(functools.partial(front_stage, devices), out_shape=(jax.Sh...  47.3 us
    pallas_call x1, Pallas kernels, mlp_call(): pl.pallas_call(functools.partial(mlp_stage, devices), out_shape=(jax.Shap...  38.3 us
    pallas_call x1, Pallas kernels, handed(): pl.pallas_call(handing_stage, out_shape=tuple((jax.ShapeDtypeStruct(a.sha...  20.5 us
    pallas_call x1, Pallas kernels, scan_call(): pl.pallas_call(scan_stage, out_shape=(jax.ShapeDtypeStruct((rows, model),...  19.4 us

profile of v2, /device:TPU:0, one launch (start us, length us, event | category | flops | bytes accessed | tf_op | source)
XLA Modules:
  0.0 127.6 jit_solution(509052361817674725)
XLA Ops:
  0.6 1.3 %concatenate.3.info = s32[17]{0:T(128)} concatenate(s32[4]{0:T(128)} %bitcast.21, s32[4]{0:T(128)} %bitcast.22, s32[4]{0:T(128)} %bitcast.23, s32[4]{0:T(128)} %bitcast.24, s32[1]{0:T(128)} %bitcast.4), dimensions={0} | concatenate | bytes 136 | tf_op jit(solution)/shard_map/concatenate | solution.py:1049
  1.9 47.3 %front_stage.1 = (f32[128,3200]{1,0:T(8,128)}, f32[128,3200]{1,0:T(8,128)}, f32[128,132]{1,0:T(8,128)}, f32[16,3200]{1,0:T(8,128)}, f32[16,3200]{1,0:T(8,128)}, ...) custom-call(s32[17]{0:T(128)} %concatenate.3.info, f32[4,3200]{1,0:T(4,128)} %taps_ref.1, f32[3200]{0:T(1024)} %conv_b_flat.1, ...), custom_call_target="tpu_custom_call" | custom-call | flops 400000000 | bytes 8000000 | tf_op jit(solution)/shard_map/front_stage/pallas_call | solution.py:562
  49.2 19.4 %scan_stage.1 = (f32[128,1600]{1,0:T(8,128)}, bf16[128,1600]{1,0:T(8,128)(2,1)}, f32[4,16,3200]{2,1,0:T(8,128)}) custom-call(s32[17]{0:T(128)} %concatenate.3.info, f32[128,3200]{1,0:T(8,128)} %get-tuple-element.19.mixed_ref, f32[128,3200]{1,0:T(8,128)} %get-tuple-element.20.step_ref, f32[128,132]{1,0:T(8,128)} %get-tuple-element.21.proj_ref, ...), custom_call_target="tpu_custom_call" | custom-call | flops 1400000000 | bytes 18000000 | tf_op jit(solution)/shard_map/scan_stage/pallas_call | solution.py:752
  68.6 38.3 %mlp_stage.1 = (bf16[1600,128]{1,0:T(8,128)(2,1)}, f32[16,3200]{1,0:T(8,128)}, bf16[3,3200]{1,0:T(4,128)(2,1)}) custom-call(s32[17]{0:T(128)} %concatenate.3.info, bf16[128,1600]{1,0:T(8,128)(2,1)} %get-tuple-element.25.normed_hbm, f32[128,1600]{1,0:T(8,128)} %get-tuple-element.26.middle_hbm, f32[4,16,3200]{2,1,0:T(8,128)} %get-tuple-element.27.final_hbm, ...), custom_call_target="tpu_custom_call" | custom-call | flops 7000000000 | bytes 16000000 | tf_op jit(solution)/shard_map/mlp_stage/pallas_call | solution.py:955
  106.9 20.5 %handing_stage.1 = (bf16[1600,128]{1,0:T(8,128)(2,1)}, f32[16,3200]{1,0:T(8,128)}, bf16[3,3200]{1,0:T(4,128)(2,1)}) custom-call(bf16[1600,128]{1,0:T(8,128)(2,1)} %get-tuple-element.29.refs_0_, f32[16,3200]{1,0:T(8,128)} %get-tuple-element.30.refs_1_, bf16[3,3200]{1,0:T(4,128)(2,1)} %get-tuple-element.31.refs_2_), custom_call_target="tpu_custom_call" | custom-call | tf_op jit(solution)/shard_map/handing_stage/pallas_call | solution.py:1012

commit v3 on v2

--- a/solution.py
+++ b/solution.py
@@ -231,13 +231,17 @@
     cache_edge_hbm,
     x_proj_hbm,
     dt_proj_hbm,
-    mixed_ref,
-    step_ref,
+    mixed_hbm,
+    step_hbm,
     proj_ref,
     enter_ref,
     last_edge_ref,
     start_ref,
     param_ref,
+    mixed_ref,
+    step_ref,
+    keep_sems,
+    since_ref,
     x_ref,
     cache_ref,
     cache_edge_ref,
@@ -320,11 +324,9 @@
     edge_sum.finish_core()
     edge_sum.start_z()
     state_sum.finish_core()
-    state_sum.start_z()
     edge_sum.finish_z()
     edge_sum.start_x()
-    state_sum.finish_z()
-    state_sum.start_x()
+    state_sum.start_z()
     edge_sum.finish_x()
     edge_sum.start_core2()
     edge_sum.finish_core2(edge3_ref)
@@ -371,14 +373,16 @@
         mixed_b[:, cols] = mixed
         mixed_ref[:, cols] = mixed.astype(jnp.float32)
 
+    state_sum.finish_z()
+    state_sum.start_x()
+    keep_mixed = pltpu.make_async_copy(mixed_ref, mixed_hbm, keep_sems.at[0])
+    keep_mixed.start()
     proj = lax.dot_general(
         mixed_b[...],
         x_proj_ref[...],
         (((1,), (1,)), ((), ())),
         preferred_element_type=jnp.float32,
     )
-    state_sum.finish_x()
-    state_sum.start_z2()
     proj_ref[...] = proj
     for s in range(STATE):
         b_wide[s] = jnp.broadcast_to(proj[:, rank + s : rank + s + 1], (rows, LANES))
@@ -403,9 +407,10 @@
         )
         suffix[:, cols] = after
 
-    state_sum.finish_z2()
-    state_sum.start_core2()
-    state_sum.finish_core2(start_ref)
+    keep_step = pltpu.make_async_copy(step_ref, step_hbm, keep_sems.at[1])
+    keep_step.start()
+    state_sum.finish_x()
+    state_sum.start_z2()
     starts_here = (last_begin >= first_pos).astype(jnp.int32)
     flag = jnp.full((1, LANES), starts_here, jnp.int32).astype(jnp.float32)
     power = (lax.broadcasted_iota(jnp.int32, (STATE, LANES), 0) + 1).astype(jnp.float32)
@@ -425,13 +430,25 @@
                 push = push * fade
                 acc[s] = acc[s] + push * b_wide[s, here, :]
         ends = jnp.concatenate([jnp.sum(a, axis=0, keepdims=True) for a in acc], axis=0)
+        end_ref[:, cols] = ends
         since = jnp.sum(since, axis=0, keepdims=True)
-        seed = jnp.exp(-(rate * since) * power) * start_ref[last_req, :, cols].astype(jnp.float32)
-        end_ref[:, cols] = ends + flag * seed
+        since_ref[:, cols] = since
         sum_ref[:, cols] = jnp.where(flag > 0.5, FAR, since)
         return carry
 
+    def one_seed(j, carry):
+        cols = pl.ds(pl.multiple_of(j * LANES, LANES), LANES)
+        rate = decay_ref[:, cols]
+        since = since_ref[:, cols]
+        seed = jnp.exp(-(rate * since) * power) * start_ref[last_req, :, cols].astype(jnp.float32)
+        end_ref[:, cols] = end_ref[:, cols] + flag * seed
+        return carry
+
     lax.fori_loop(0, inner // LANES, one_tile, 0)
+    state_sum.finish_z2()
+    state_sum.start_core2()
+    state_sum.finish_core2(start_ref)
+    lax.fori_loop(0, inner // LANES, one_seed, 0)
     power16 = (lax.broadcasted_iota(jnp.int32, (STATE, LANES), 0) + 1).astype(jnp.float32)
     half = half_width(inner)
     tiles = half // LANES
@@ -552,6 +569,8 @@
             + jnp.dot(hot_rows(near_at, 16), halo_ref[:, cols], preferred_element_type=jnp.float32)
             + jnp.dot(hot_rows(far_at, 16), edge_ref[:, cols], preferred_element_type=jnp.float32)
         )
+    keep_mixed.wait()
+    keep_step.wait()
 
 
 def front_call(devices, info, args, rows, inner, proj_width, requests):
@@ -571,8 +590,12 @@
             jax.ShapeDtypeStruct((16, inner), f32),
         ),
         in_specs=[sspec()] + [vspec()] * 6 + [hspec()] * (len(args) - 6),
-        out_specs=tuple([vspec()] * 7),
+        out_specs=tuple([hspec()] * 2 + [vspec()] * 5),
         scratch_shapes=[
+            VMEM((rows, inner), f32),
+            VMEM((rows, inner), f32),
+            pltpu.SemaphoreType.DMA((2,)),
+            VMEM((1, inner), f32),
             VMEM((rows, inner), bf16),
             VMEM((STATE, inner), f32),
             VMEM((EDGE, inner), bf16),
@@ -614,8 +637,8 @@
 
 def scan_stage(
     info,
-    mixed_ref,
-    step_ref,
+    mixed_hbm,
+    step_hbm,
     proj_ref,
     enter_ref,
     start_ref,
@@ -624,7 +647,12 @@
     out_w_hbm,
     middle_ref,
     normed_ref,
+    final_hbm,
+    mixed_ref,
+    step_ref,
     final_ref,
+    block_sems,
+    final_sem,
     bc_wide,
     y_ref,
     ssm_b,
@@ -637,6 +665,20 @@
     width = col_block(inner)
     tiles = width // LANES
     rank = proj_ref.shape[1] - 2 * STATE
+    width = col_block(step_ref.shape[1])
+
+    def block_copies(g):
+        cols = pl.ds(pl.multiple_of(g * width, LANES), width)
+        return (
+            pltpu.make_async_copy(
+                mixed_hbm.at[:, cols], mixed_ref.at[:, cols], block_sems.at[0, g]
+            ),
+            pltpu.make_async_copy(step_hbm.at[:, cols], step_ref.at[:, cols], block_sems.at[1, g]),
+        )
+
+    for g in range(step_ref.shape[1] // width):
+        for copy in block_copies(g):
+            copy.start()
     fetch = pltpu.make_async_copy(out_w_hbm, out_w, w_sem)
     fetch.start()
     fetch_hidden = pltpu.make_async_copy(hidden_hbm, hidden_ref, hidden_sem)
@@ -668,6 +710,8 @@
         return outs, tuple(new)
 
     def one_block(g, carry):
+        for copy in block_copies(g):
+            copy.wait()
         base = pl.multiple_of(g * width, LANES)
         tile_cols = [pl.ds(pl.multiple_of(base + j * LANES, LANES), LANES) for j in range(tiles)]
         rates = [-decay_ref[:, c] * power for c in tile_cols]
@@ -732,6 +776,8 @@
         return carry
 
     lax.fori_loop(0, inner // width, one_block, 0)
+    keep_final = pltpu.make_async_copy(final_ref, final_hbm, final_sem)
+    keep_final.start()
     fetch.wait()
     fetch_hidden.wait()
     middle = jnp.transpose(hidden_ref[...].astype(jnp.float32))
@@ -745,6 +791,7 @@
     middle_ref[...] = middle
     scale = lax.rsqrt(jnp.mean(middle * middle, axis=1, keepdims=True) + NORM_EPS)
     normed_ref[...] = (middle * scale * param_ref[8:9, :model]).astype(jnp.bfloat16)
+    keep_final.wait()
 
 
 def scan_call(info, args, out_w, rows, inner, model, requests):
@@ -756,9 +803,14 @@
             jax.ShapeDtypeStruct((rows, model), jnp.bfloat16),
             jax.ShapeDtypeStruct((requests, STATE, inner), f32),
         ),
-        in_specs=[sspec()] + [vspec()] * (len(args) - 1) + [hspec()] * 2,
-        out_specs=tuple([vspec()] * 3),
+        in_specs=[sspec()] + [hspec()] * 2 + [vspec()] * (len(args) - 3) + [hspec()] * 2,
+        out_specs=tuple([vspec()] * 2 + [hspec()]),
         scratch_shapes=[
+            VMEM((rows, inner), f32),
+            VMEM((rows, inner), f32),
+            VMEM((requests, STATE, inner), f32),
+            pltpu.SemaphoreType.DMA((2, inner // col_block(inner))),
+            pltpu.SemaphoreType.DMA,
             VMEM((rows, 2 * STATE, LANES), f32),
             VMEM((rows, inner), f32),
             VMEM((rows, inner), jnp.bfloat16),
@@ -887,36 +939,36 @@
     finals.finish_core()
     finals.start_z()
     edges.finish_core()
-    for copy in fetches[3:]:
-        copy.wait()
     up_a.wait_recv()
     up_a2.start()
     down_b.wait_recv()
     down_b2.start()
+    for copy in fetches[3:]:
+        copy.wait()
+    out1[...] = hidden_units(near1[...]).astype(jnp.bfloat16)
     up_b.start()
     down_a.start()
-    out1[...] = hidden_units(near1[...]).astype(jnp.bfloat16)
-    finals.finish_z()
-    finals.start_x()
-    edges.start_z()
     up_a2.wait_recv()
     down_b2.wait_recv()
     far_out[...] = hidden_units(far[...]).astype(jnp.bfloat16)
     far_up.start()
     far_down.start()
-    back_down.start()
-    back_up.start()
+    finals.finish_z()
+    finals.start_x()
+    edges.start_z()
     up_b.wait_recv()
     down_a.wait_recv()
     own_out[...] = hidden_units(near2[...])
-    finals.finish_x()
-    finals.start_z2()
+    back_down.start()
+    back_up.start()
     far_down.wait_recv()
     out2[first] = (own_out[first] + far_in[second].astype(jnp.float32)).astype(jnp.bfloat16)
     last_down.start()
     far_up.wait_recv()
     out2[second] = (own_out[second] + far_in[first].astype(jnp.float32)).astype(jnp.bfloat16)
     last_up.start()
+    finals.finish_x()
+    finals.start_z2()
     edges.finish_z()
     edges.start_x()
     own_out[...] = hidden_units(normed_ref[...]) + middle_ref[...]
@@ -997,24 +1049,17 @@
 
 
 def handing_stage(*refs):
-    count = (len(refs) - 1) // 2
-    sems = refs[-1]
-    copies = [
-        pltpu.make_async_copy(refs[i], refs[count + i], sems.at[i]) for i in range(count)
-    ]
-    for copy in copies:
-        copy.start()
-    for copy in copies:
-        copy.wait()
+    count = len(refs) // 2
+    for i in range(count):
+        refs[count + i][...] = refs[i][...]
 
 
 def handed(*arrays):
     return pl.pallas_call(
         handing_stage,
         out_shape=tuple(jax.ShapeDtypeStruct(a.shape, a.dtype) for a in arrays),
-        in_specs=[pl.BlockSpec(memory_space=pl.ANY)] * len(arrays),
-        out_specs=tuple([hspec()] * len(arrays)),
-        scratch_shapes=[pltpu.SemaphoreType.DMA((len(arrays),))],
+        in_specs=[vspec()] * len(arrays),
+        out_specs=tuple([vspec()] * len(arrays)),
         name="handing_stage",
     )(*arrays)
 

time: 128 us -> 107 us (0.84)
  Pallas kernels: 125 us -> 105 us
    pallas_call x1, Pallas kernels: 20.5 us -> 1.95 us  [handed(): pl.pallas_call(handing_stage, out_shape=tuple((jax.ShapeDtypeStruct(a.sha...]
where the time goes in v3:
time: 107 us
  Pallas kernels  105 us (98%)
  local copies, waits for them, and re-layouts  1.3 us (1%)
    pallas_call x1, Pallas kernels, front_call(): pl.pallas_call(functools.partial(front_stage, devices), out_shape=(jax.Sh...  46.3 us
    pallas_call x1, Pallas kernels, mlp_call(): pl.pallas_call(functools.partial(mlp_stage, devices), out_shape=(jax.Shap...  38.4 us
    pallas_call x1, Pallas kernels, scan_call(): pl.pallas_call(scan_stage, out_shape=(jax.ShapeDtypeStruct((rows, model),...  18.5 us

profile of v3, /device:TPU:0, one launch (start us, length us, event | category | flops | bytes accessed | tf_op | source)
XLA Modules:
  0.0 107.2 jit_solution(8695178943374273775)
XLA Ops:
  0.6 1.3 %concatenate.3.info = s32[17]{0:T(128)} concatenate(s32[4]{0:T(128)} %bitcast.21, s32[4]{0:T(128)} %bitcast.22, s32[4]{0:T(128)} %bitcast.23, s32[4]{0:T(128)} %bitcast.24, s32[1]{0:T(128)} %bitcast.4), dimensions={0} | concatenate | bytes 136 | tf_op jit(solution)/shard_map/concatenate | solution.py:1094
  1.9 46.3 %front_stage.1 = (f32[128,3200]{1,0:T(8,128)}, f32[128,3200]{1,0:T(8,128)}, f32[128,132]{1,0:T(8,128)}, f32[16,3200]{1,0:T(8,128)}, f32[16,3200]{1,0:T(8,128)}, ...) custom-call(s32[17]{0:T(128)} %concatenate.3.info, f32[4,3200]{1,0:T(4,128)} %taps_ref.1, f32[3200]{0:T(1024)} %conv_b_flat.1, ...), custom_call_target="tpu_custom_call" | custom-call | flops 400000000 | bytes 8000000 | tf_op jit(solution)/shard_map/front_stage/pallas_call | solution.py:581
  48.2 18.5 %scan_stage.1 = (f32[128,1600]{1,0:T(8,128)}, bf16[128,1600]{1,0:T(8,128)(2,1)}, f32[4,16,3200]{2,1,0:T(8,128)}) custom-call(s32[17]{0:T(128)} %concatenate.3.info, f32[128,3200]{1,0:T(8,128)} %get-tuple-element.19.mixed_hbm, f32[128,3200]{1,0:T(8,128)} %get-tuple-element.20.step_hbm, f32[128,132]{1,0:T(8,128)} %get-tuple-element.21.proj_ref, ...), custom_call_target="tpu_custom_call" | custom-call | flops 1400000000 | bytes 18000000 | tf_op jit(solution)/shard_map/scan_stage/pallas_call | solution.py:799
  66.8 38.4 %mlp_stage.1 = (bf16[1600,128]{1,0:T(8,128)(2,1)}, f32[16,3200]{1,0:T(8,128)}, bf16[3,3200]{1,0:T(4,128)(2,1)}) custom-call(s32[17]{0:T(128)} %concatenate.3.info, bf16[128,1600]{1,0:T(8,128)(2,1)} %get-tuple-element.25.normed_hbm, f32[128,1600]{1,0:T(8,128)} %get-tuple-element.26.middle_hbm, f32[4,16,3200]{2,1,0:T(8,128)} %get-tuple-element.27.final_hbm, ...), custom_call_target="tpu_custom_call" | custom-call | flops 7000000000 | bytes 16000000 | tf_op jit(solution)/shard_map/mlp_stage/pallas_call | solution.py:1007
  105.2 1.9 %handing_stage.1 = (bf16[1600,128]{1,0:T(8,128)(2,1)}, f32[16,3200]{1,0:T(8,128)}, bf16[3,3200]{1,0:T(4,128)(2,1)}) custom-call(bf16[1600,128]{1,0:T(8,128)(2,1)} %get-tuple-element.29.refs_0_, f32[16,3200]{1,0:T(8,128)} %get-tuple-element.30.refs_1_, bf16[3,3200]{1,0:T(4,128)(2,1)} %get-tuple-element.31.refs_2_), custom_call_target="tpu_custom_call" | custom-call | tf_op jit(solution)/shard_map/handing_stage/pallas_call | solution.py:1058

commit v4 on v3

--- a/solution.py
+++ b/solution.py
@@ -39,6 +39,10 @@
 def layout_of(devices):
     depth = 4 if devices >= 32 else 2
     return devices // (2 * depth), depth
+
+
+def padded(width):
+    return -(-width // LANES) * LANES
 
 
 def half_width(inner):
@@ -217,6 +221,59 @@
     return begin, low, high, fresh, ends
 
 
+def summed(ones, step):
+    high = step.astype(jnp.bfloat16)
+    rest = step - high.astype(jnp.float32)
+    mid = rest.astype(jnp.bfloat16)
+    low = (rest - mid.astype(jnp.float32)).astype(jnp.bfloat16)
+    return (
+        jnp.dot(ones, high, preferred_element_type=jnp.float32)
+        + jnp.dot(ones, mid, preferred_element_type=jnp.float32)
+        + jnp.dot(ones, low, preferred_element_type=jnp.float32)
+    )
+
+
+def local_scan(g, width, rows, mixed_ref, step_ref, decay_ref, reset_ref, bc_wide, y_ref):
+    tiles = width // LANES
+    power = (lax.broadcasted_iota(jnp.int32, (8, LANES), 0) + 1).astype(jnp.float32)
+    tile_cols = [
+        pl.ds(pl.multiple_of(g * width + j * LANES, LANES), LANES) for j in range(tiles)
+    ]
+    decays = [decay_ref[:, c] for c in tile_cols]
+    rates = [-d * power for d in decays]
+
+    def eight(block, state):
+        row = pl.multiple_of(block * 8, 8)
+        here = pl.ds(row, 8)
+        reset = reset_ref[here, :]
+        step = [step_ref[here, c] for c in tile_cols]
+        push = [s * mixed_ref[here, c] for s, c in zip(step, tile_cols)]
+        step = [s + reset for s in step]
+        fade8 = [jnp.exp(-8.0 * (s * d)) for s, d in zip(step, decays)]
+        kept = [[] for _ in range(tiles)]
+        for i in range(8):
+            b_low, b_high = bc_wide[row + i, 0:8], bc_wide[row + i, 8:16]
+            c_low, c_high = bc_wide[row + i, 16:24], bc_wide[row + i, 24:32]
+            new = []
+            for j in range(tiles):
+                s_row, p_row, f_row = (
+                    jnp.broadcast_to(part[j][i : i + 1], (8, LANES))
+                    for part in (step, push, fade8)
+                )
+                d_low = jnp.exp(s_row * rates[j])
+                low = d_low * state[2 * j] + b_low * p_row
+                high = d_low * f_row * state[2 * j + 1] + b_high * p_row
+                new += [low, high]
+                kept[j].append(jnp.sum(c_low * low + c_high * high, axis=0, keepdims=True))
+            state = tuple(new)
+        for j in range(tiles):
+            y_ref[here, tile_cols[j]] = jnp.concatenate(kept[j], axis=0)
+        return state
+
+    zero = jnp.zeros((8, LANES), jnp.float32)
+    lax.fori_loop(0, rows // 8, eight, (zero,) * (2 * tiles))
+
+
 def front_stage(
     devices,
     info,
@@ -233,6 +290,8 @@
     dt_proj_hbm,
     mixed_hbm,
     step_hbm,
+    y_hbm,
+    pre_hbm,
     proj_ref,
     enter_ref,
     last_edge_ref,
@@ -242,6 +301,11 @@
     step_ref,
     keep_sems,
     since_ref,
+    y_ref,
+    pre_ref,
+    bc_wide,
+    reset_ref,
+    block_sems,
     x_ref,
     cache_ref,
     cache_edge_ref,
@@ -396,16 +460,7 @@
         v = v + dt_bias_ref[:, cols]
         step = jnp.maximum(v, 0.0) + jnp.log1p(jnp.exp(-jnp.abs(v)))
         step_ref[:, cols] = step
-        high = step.astype(jnp.bfloat16)
-        rest = step - high.astype(jnp.float32)
-        mid = rest.astype(jnp.bfloat16)
-        low = (rest - mid.astype(jnp.float32)).astype(jnp.bfloat16)
-        after = (
-            jnp.dot(later, high, preferred_element_type=jnp.float32)
-            + jnp.dot(later, mid, preferred_element_type=jnp.float32)
-            + jnp.dot(later, low, preferred_element_type=jnp.float32)
-        )
-        suffix[:, cols] = after
+        suffix[:, cols] = summed(later, step)
 
     keep_step = pltpu.make_async_copy(step_ref, step_hbm, keep_sems.at[1])
     keep_step.start()
@@ -462,6 +517,41 @@
     ]
     for copy in pair:
         copy.start()
+    reset_ref[...] = jnp.where(offset == 0, FAR, 0.0)
+    turned = jnp.transpose(proj_ref[:, rank : rank + 2 * STATE])
+    for t in range(rows):
+        bc_wide[t] = jnp.broadcast_to(turned[:, t : t + 1], (2 * STATE, LANES))
+    at_row = first_pos + row_id
+    at_col = first_pos + col_id
+    begin_row = jnp.zeros((rows, rows), jnp.int32)
+    begin_col = jnp.zeros((rows, rows), jnp.int32)
+    for r in range(1, requests):
+        begin_row = jnp.where(at_row >= marks[r][0], marks[r][0], begin_row)
+        begin_col = jnp.where(at_col >= marks[r][0], marks[r][0], begin_col)
+    upto = ((col_id <= row_id) & (begin_row == begin_col)).astype(jnp.float32)
+    upto = upto.astype(jnp.bfloat16)
+    blocks = inner // width
+    cuts = [0, -(-blocks // 5), -(-3 * blocks // 5), blocks]
+
+    def block_keeps(g):
+        cols = pl.ds(pl.multiple_of(g * width, LANES), width)
+        return (
+            pltpu.make_async_copy(y_ref.at[:, cols], y_hbm.at[:, cols], block_sems.at[0, g]),
+            pltpu.make_async_copy(pre_ref.at[:, cols], pre_hbm.at[:, cols], block_sems.at[1, g]),
+        )
+
+    def scan_block(g, carry):
+        cols = pl.ds(pl.multiple_of(g * width, LANES), width)
+        local_scan(
+            g, width, rows, mixed_ref, step_ref, decay_ref, reset_ref, bc_wide, y_ref
+        )
+        y_ref[:, cols] = y_ref[:, cols] + param_ref[7:8, cols] * mixed_ref[:, cols]
+        pre_ref[:, cols] = summed(upto, step_ref[:, cols])
+        for copy in block_keeps(g):
+            copy.start()
+        return carry
+
+    lax.fori_loop(cuts[0], cuts[1], scan_block, 0)
     across, depth = layout_of(devices)
     first_core = core == 0
 
@@ -491,6 +581,7 @@
         copies.append(send(z_s.at[0], z_s.at[d + 1], pre_sems, 3 + 2 * d, peer))
     for copy in copies:
         copy.start()
+    lax.fori_loop(cuts[1], cuts[2], scan_block, 0)
     for copy in copies:
         copy.wait()
     prefix = []
@@ -520,6 +611,7 @@
         copies.append(send(x_s.at[0], x_s.at[d + 1], pre_sems, first + 1 + 2 * d, peer))
     for copy in copies:
         copy.start()
+    lax.fori_loop(cuts[2], cuts[3], scan_block, 0)
     for copy in copies:
         copy.wait()
     for j in range(tiles):
@@ -571,6 +663,9 @@
         )
     keep_mixed.wait()
     keep_step.wait()
+    for g in range(blocks):
+        for copy in block_keeps(g):
+            copy.wait()
 
 
 def front_call(devices, info, args, rows, inner, proj_width, requests):
@@ -583,6 +678,8 @@
         out_shape=(
             jax.ShapeDtypeStruct((rows, inner), f32),
             jax.ShapeDtypeStruct((rows, inner), f32),
+            jax.ShapeDtypeStruct((rows, inner), f32),
+            jax.ShapeDtypeStruct((rows, inner), f32),
             jax.ShapeDtypeStruct((rows, proj_width), f32),
             jax.ShapeDtypeStruct((STATE, inner), f32),
             jax.ShapeDtypeStruct((16, inner), f32),
@@ -590,12 +687,17 @@
             jax.ShapeDtypeStruct((16, inner), f32),
         ),
         in_specs=[sspec()] + [vspec()] * 6 + [hspec()] * (len(args) - 6),
-        out_specs=tuple([hspec()] * 2 + [vspec()] * 5),
+        out_specs=tuple([hspec()] * 4 + [vspec()] * 5),
         scratch_shapes=[
             VMEM((rows, inner), f32),
             VMEM((rows, inner), f32),
             pltpu.SemaphoreType.DMA((2,)),
             VMEM((1, inner), f32),
+            VMEM((rows, inner), f32),
+            VMEM((rows, inner), f32),
+            VMEM((rows, 2 * STATE, LANES), f32),
+            VMEM((rows, LANES), f32),
+            pltpu.SemaphoreType.DMA((2, inner // col_block(inner))),
             VMEM((rows, inner), bf16),
             VMEM((STATE, inner), f32),
             VMEM((EDGE, inner), bf16),
@@ -635,10 +737,12 @@
     )(info, *args)
 
 
-def scan_stage(
+def join_stage(
     info,
+    y_hbm,
+    pre_hbm,
+    step_hbm,
     mixed_hbm,
-    step_hbm,
     proj_ref,
     enter_ref,
     start_ref,
@@ -648,131 +752,147 @@
     middle_ref,
     normed_ref,
     final_hbm,
+    y_ref,
+    pre_ref,
+    step_ref,
     mixed_ref,
-    step_ref,
     final_ref,
     block_sems,
+    extra_sems,
     final_sem,
-    bc_wide,
-    y_ref,
+    b_wide,
+    c_wide,
     ssm_b,
     out_w,
     hidden_ref,
     w_sem,
     hidden_sem,
 ):
-    rows, inner = mixed_ref.shape
+    rows, inner = y_ref.shape
     width = col_block(inner)
     tiles = width // LANES
+    requests = final_ref.shape[0]
     rank = proj_ref.shape[1] - 2 * STATE
-    width = col_block(step_ref.shape[1])
+    model = hidden_ref.shape[0]
+    decay_ref = param_ref.at[pl.ds(6, 1)]
+    span = min(64, rows)
+    marks = [segment(info, r, rows) for r in range(requests)]
+    any_end = marks[0][4]
+    for r in range(1, requests):
+        any_end = any_end | marks[r][4]
 
     def block_copies(g):
         cols = pl.ds(pl.multiple_of(g * width, LANES), width)
         return (
-            pltpu.make_async_copy(
-                mixed_hbm.at[:, cols], mixed_ref.at[:, cols], block_sems.at[0, g]
-            ),
-            pltpu.make_async_copy(step_hbm.at[:, cols], step_ref.at[:, cols], block_sems.at[1, g]),
-        )
-
-    for g in range(step_ref.shape[1] // width):
+            pltpu.make_async_copy(pre_hbm.at[:, cols], pre_ref.at[:, cols], block_sems.at[0, g]),
+            pltpu.make_async_copy(y_hbm.at[:, cols], y_ref.at[:, cols], block_sems.at[1, g]),
+        )
+
+    extra = (
+        pltpu.make_async_copy(step_hbm, step_ref, extra_sems.at[0]),
+        pltpu.make_async_copy(mixed_hbm, mixed_ref, extra_sems.at[1]),
+    )
+    for g in range(inner // width):
         for copy in block_copies(g):
             copy.start()
+
+    @pl.when(any_end)
+    def _():
+        for copy in extra:
+            copy.start()
+
     fetch = pltpu.make_async_copy(out_w_hbm, out_w, w_sem)
     fetch.start()
     fetch_hidden = pltpu.make_async_copy(hidden_hbm, hidden_ref, hidden_sem)
     fetch_hidden.start()
-    model = hidden_ref.shape[0]
-    decay_ref = param_ref.at[pl.ds(6, 1)]
-    skip_ref = param_ref.at[pl.ds(7, 1)]
-
-    turned = jnp.transpose(proj_ref[:, rank : rank + 2 * STATE])
-    for t in range(rows):
-        bc_wide[t] = jnp.broadcast_to(turned[:, t : t + 1], (2 * STATE, LANES))
+    proj = proj_ref[...]
+    for s in range(STATE):
+        at = rank + STATE + s
+        c_wide[s] = jnp.broadcast_to(proj[:, at : at + 1], (rows, LANES))
     final_ref[...] = jnp.zeros_like(final_ref)
-    power = (lax.broadcasted_iota(jnp.int32, (8, LANES), 0) + 1).astype(jnp.float32)
-
-    def wide_step(t, i, step, push, fade8, state, rates):
-        b_low, b_high = bc_wide[t, 0:8], bc_wide[t, 8:16]
-        c_low, c_high = bc_wide[t, 16:24], bc_wide[t, 24:32]
-        outs, new = [], []
-        for j in range(tiles):
-            s_row, p_row, f_row = (
-                jnp.broadcast_to(part[j][i : i + 1], (8, LANES)) for part in (step, push, fade8)
-            )
-            d_low = jnp.exp(s_row * rates[j])
-            d_high = d_low * f_row
-            low = d_low * state[2 * j] + b_low * p_row
-            high = d_high * state[2 * j + 1] + b_high * p_row
-            new += [low, high]
-            outs.append(jnp.sum(c_low * low + c_high * high, axis=0, keepdims=True))
-        return outs, tuple(new)
+
+    @pl.when(any_end)
+    def _():
+        for s in range(STATE):
+            b_wide[s] = jnp.broadcast_to(proj[:, rank + s : rank + s + 1], (rows, LANES))
+        for copy in extra:
+            copy.wait()
+
+    power = (lax.broadcasted_iota(jnp.int32, (STATE, LANES), 0) + 1).astype(jnp.float32)
+    tile_row = lax.broadcasted_iota(jnp.int32, (8, LANES), 0)
 
     def one_block(g, carry):
         for copy in block_copies(g):
             copy.wait()
-        base = pl.multiple_of(g * width, LANES)
-        tile_cols = [pl.ds(pl.multiple_of(base + j * LANES, LANES), LANES) for j in range(tiles)]
-        rates = [-decay_ref[:, c] * power for c in tile_cols]
-        decays = [decay_ref[:, c] for c in tile_cols]
-
-        def load(row, count):
-            step = [step_ref[pl.ds(row, count), c] for c in tile_cols]
-            push = [s * mixed_ref[pl.ds(row, count), c] for s, c in zip(step, tile_cols)]
-            fade8 = [jnp.exp(-8.0 * (s * d)) for s, d in zip(step, decays)]
-            return step, push, fade8
-
-        def eight(block, state, limits=None):
-            row = pl.multiple_of(block * 8, 8)
-            step, push, fade8 = load(row, 8)
-            kept = [[] for _ in range(tiles)]
-            for i in range(8):
-                outs, new = wide_step(row + i, i, step, push, fade8, state, rates)
-                if limits is not None:
-                    active = (row + i >= limits[0]) & (row + i < limits[1])
-                    new = tuple(jnp.where(active, a, b) for a, b in zip(new, state))
-                state = new
-                for j in range(tiles):
-                    kept[j].append(outs[j])
-            for j in range(tiles):
-                y = jnp.concatenate(kept[j], axis=0)
-                if limits is not None:
-                    at = row + lax.broadcasted_iota(jnp.int32, (8, LANES), 0)
-                    y = jnp.where(
-                        (at >= limits[0]) & (at < limits[1]), y, y_ref[pl.ds(row, 8), tile_cols[j]]
-                    )
-                y_ref[pl.ds(row, 8), tile_cols[j]] = y
-            return state
-
-        for r in range(final_ref.shape[0]):
-            _, begin, end, new, ends = segment(info, r, rows)
-
-            @pl.when(end > begin)
+        for r in range(requests):
+            _, low, high, new, ends = marks[r]
+            spans = (low // span, (high + span - 1) // span)
+
+            @pl.when(high > low)
             def _():
-                state = []
-                for c in tile_cols:
-                    for half in (pl.ds(0, 8), pl.ds(8, 8)):
-                        old = enter_ref[half, c]
-                        seed = start_ref[r, half, c].astype(jnp.float32)
-                        state.append(jnp.where(new, seed, old))
-                state = tuple(state)
-                part = functools.partial(eight, limits=(begin, end))
-                low, low_up, high = begin // 8, (begin + 7) // 8, end // 8
-                state = lax.fori_loop(low, low_up, part, state)
-                state = lax.fori_loop(low_up, jnp.maximum(high, low_up), eight, state)
-                tail = jnp.where((high >= low_up) & (end % 8 > 0), high + 1, high)
-                state = lax.fori_loop(high, tail, part, state)
-
-                @pl.when(ends)
-                def _():
-                    for j, c in enumerate(tile_cols):
-                        final_ref[r, pl.ds(0, 8), c] = state[2 * j]
-                        final_ref[r, pl.ds(8, 8), c] = state[2 * j + 1]
-
-        y = y_ref[:, pl.ds(base, width)]
-        y = y + skip_ref[:, pl.ds(base, width)] * mixed_ref[:, pl.ds(base, width)]
-        ssm_b[:, pl.ds(base, width)] = y.astype(jnp.bfloat16)
+                def one_tile(j, inside):
+                    cols = pl.ds(pl.multiple_of(g * width + j * LANES, LANES), LANES)
+                    decay = decay_ref[:, cols]
+                    seed = start_ref[r, :, cols].astype(jnp.float32)
+                    origin = jnp.where(new, seed, enter_ref[:, cols])
+                    wide = [jnp.broadcast_to(origin[s : s + 1], (8, LANES)) for s in range(STATE)]
+
+                    def parts(q):
+                        found = []
+                        for k in range(span // 8):
+                            row = pl.multiple_of(q * span + k * 8, 8)
+                            at = row + tile_row
+                            found.append((pl.ds(row, 8), (at >= low) & (at < high)))
+                        return found
+
+                    def add(q, done):
+                        for here, inside in parts(q):
+                            fade = jnp.exp(-decay * pre_ref[here, cols])
+                            total = c_wide[STATE - 1, here, :] * wide[STATE - 1]
+                            for s in range(STATE - 2, -1, -1):
+                                total = total * fade + c_wide[s, here, :] * wide[s]
+                            y = y_ref[here, cols]
+                            y_ref[here, cols] = jnp.where(inside, y + total * fade, y)
+                        return done
+
+                    lax.fori_loop(spans[0], spans[1], add, 0)
+
+                    @pl.when(ends)
+                    def _():
+                        def count(q, whole):
+                            for here, inside in parts(q):
+                                whole = whole + jnp.where(inside, step_ref[here, cols], 0.0)
+                            return whole
+
+                        whole = lax.fori_loop(
+                            spans[0], spans[1], count, jnp.zeros((8, LANES), jnp.float32)
+                        )
+                        whole = jnp.sum(whole, axis=0, keepdims=True)
+
+                        def gather(q, acc):
+                            acc = list(acc)
+                            for here, inside in parts(q):
+                                left = jnp.where(inside, whole - pre_ref[here, cols], 0.0)
+                                fade = jnp.exp(-decay * left)
+                                push = step_ref[here, cols] * mixed_ref[here, cols]
+                                push = jnp.where(inside, push, 0.0)
+                                for s in range(STATE):
+                                    push = push * fade
+                                    acc[s] = acc[s] + push * b_wide[s, here, :]
+                            return tuple(acc)
+
+                        zero = jnp.zeros((8, LANES), jnp.float32)
+                        acc = lax.fori_loop(spans[0], spans[1], gather, (zero,) * STATE)
+                        own = [jnp.sum(a, axis=0, keepdims=True) for a in acc]
+                        own = jnp.concatenate(own, axis=0)
+                        final_ref[r, :, cols] = own + jnp.exp(-(decay * whole) * power) * origin
+
+                    return inside
+
+                lax.fori_loop(0, tiles, one_tile, 0)
+
+        cols = pl.ds(pl.multiple_of(g * width, LANES), width)
+        ssm_b[:, cols] = y_ref[:, cols].astype(jnp.bfloat16)
         return carry
 
     lax.fori_loop(0, inner // width, one_block, 0)
@@ -790,29 +910,35 @@
         )
     middle_ref[...] = middle
     scale = lax.rsqrt(jnp.mean(middle * middle, axis=1, keepdims=True) + NORM_EPS)
-    normed_ref[...] = (middle * scale * param_ref[8:9, :model]).astype(jnp.bfloat16)
+    normed = (middle * scale * param_ref[8:9, :model]).astype(jnp.bfloat16)
+    if normed_ref.shape[1] > model:
+        normed_ref[...] = jnp.zeros_like(normed_ref)
+    normed_ref[:, :model] = normed
     keep_final.wait()
 
 
-def scan_call(info, args, out_w, rows, inner, model, requests):
+def join_call(info, args, out_w, rows, inner, model, requests):
     f32 = jnp.float32
     return pl.pallas_call(
-        scan_stage,
+        join_stage,
         out_shape=(
             jax.ShapeDtypeStruct((rows, model), f32),
-            jax.ShapeDtypeStruct((rows, model), jnp.bfloat16),
+            jax.ShapeDtypeStruct((rows, padded(model)), jnp.bfloat16),
             jax.ShapeDtypeStruct((requests, STATE, inner), f32),
         ),
-        in_specs=[sspec()] + [hspec()] * 2 + [vspec()] * (len(args) - 3) + [hspec()] * 2,
+        in_specs=[sspec()] + [hspec()] * 4 + [vspec()] * (len(args) - 5) + [hspec()] * 2,
         out_specs=tuple([vspec()] * 2 + [hspec()]),
         scratch_shapes=[
             VMEM((rows, inner), f32),
             VMEM((rows, inner), f32),
+            VMEM((rows, inner), f32),
+            VMEM((rows, inner), f32),
             VMEM((requests, STATE, inner), f32),
             pltpu.SemaphoreType.DMA((2, inner // col_block(inner))),
+            pltpu.SemaphoreType.DMA((2,)),
             pltpu.SemaphoreType.DMA,
-            VMEM((rows, 2 * STATE, LANES), f32),
-            VMEM((rows, inner), f32),
+            VMEM((STATE, rows, LANES), f32),
+            VMEM((STATE, rows, LANES), f32),
             VMEM((rows, inner), jnp.bfloat16),
             VMEM((model, inner), jnp.bfloat16),
             VMEM((model, rows), jnp.bfloat16),
@@ -823,7 +949,7 @@
         cost_estimate=pl.CostEstimate(
             flops=1_400_000_000, bytes_accessed=18_000_000, transcendentals=4_000_000
         ),
-        name="scan_stage",
+        name="join_stage",
     )(info, *args, out_w)
 
 
@@ -863,7 +989,7 @@
     full_edge,
     *spread_refs,
 ):
-    rows, model = normed_ref.shape
+    rows, model = middle_ref.shape
     half = rows // 2
     inner = final_ref.shape[2]
     requests = final_ref.shape[0]
@@ -901,22 +1027,30 @@
             device_id_type=MESH_ID,
         )
 
+    piece = [pl.ds(i * (half // 2), half // 2) for i in range(4)]
     first, second = pl.ds(0, half), pl.ds(half, half)
-    up_a = hop(normed_ref.at[first], near1.at[first], 0, above)
-    down_b = hop(normed_ref.at[second], near1.at[second], 1, below)
-    up_a2 = hop(near1.at[first], far.at[first], 2, above)
-    down_b2 = hop(near1.at[second], far.at[second], 3, below)
-    up_b = hop(normed_ref.at[second], near2.at[first], 4, above)
-    down_a = hop(normed_ref.at[first], near2.at[second], 5, below)
-    far_up = hop(far_out.at[first], far_in.at[first], 6, above)
-    far_down = hop(far_out.at[second], far_in.at[second], 7, below)
-    back_down = hop(out1.at[first], high_in.at[first], 8, below)
-    back_up = hop(out1.at[second], low_in.at[second], 9, above)
-    last_down = hop(out2.at[first], high_in.at[second], 10, below)
-    last_up = hop(out2.at[second], low_in.at[first], 11, above)
+    toward = [above, above, below, below]
+    out_hops = [hop(normed_ref.at[piece[i]], near1.at[piece[i]], i, toward[i]) for i in range(4)]
+    on_hops = [hop(near1.at[piece[i]], far.at[piece[i]], 4 + i, toward[i]) for i in range(4)]
+    up_b = hop(normed_ref.at[second], near2.at[first], 8, above)
+    down_a = hop(normed_ref.at[first], near2.at[second], 9, below)
+    far_hops = [hop(far_out.at[piece[i]], far_in.at[piece[i]], 10 + i, toward[i]) for i in range(4)]
+    back_down = hop(out1.at[first], high_in.at[first], 14, below)
+    back_up = hop(out1.at[second], low_in.at[second], 15, above)
+    swap = [2, 3, 0, 1]
+    last_hops = [
+        hop(
+            out2.at[piece[swap[i]]],
+            (low_in if i < 2 else high_in).at[piece[i]],
+            16 + i,
+            toward[i],
+        )
+        for i in range(4)
+    ]
+    order = (0, 2, 1, 3)
     fetches[0].wait()
-    up_a.start()
-    down_b.start()
+    for i in order:
+        out_hops[i].start()
     per = len(Spread.scratch(devices, inner, 1, False))
     finals = Spread(devices, inner, requests, True, spread_refs[:per])
     edges = Spread(devices, inner, 1, False, spread_refs[per:])
@@ -939,39 +1073,38 @@
     finals.finish_core()
     finals.start_z()
     edges.finish_core()
-    up_a.wait_recv()
-    up_a2.start()
-    down_b.wait_recv()
-    down_b2.start()
+    for i in order:
+        out_hops[i].wait_recv()
+        on_hops[i].start()
+    up_b.start()
+    down_a.start()
     for copy in fetches[3:]:
         copy.wait()
-    out1[...] = hidden_units(near1[...]).astype(jnp.bfloat16)
-    up_b.start()
-    down_a.start()
-    up_a2.wait_recv()
-    down_b2.wait_recv()
-    far_out[...] = hidden_units(far[...]).astype(jnp.bfloat16)
-    far_up.start()
-    far_down.start()
+    out1[:, :model] = hidden_units(near1[:, :model]).astype(jnp.bfloat16)
+    for i in order:
+        on_hops[i].wait_recv()
+    far_out[:, :model] = hidden_units(far[:, :model]).astype(jnp.bfloat16)
+    for i in order:
+        far_hops[i].start()
     finals.finish_z()
     finals.start_x()
     edges.start_z()
     up_b.wait_recv()
     down_a.wait_recv()
-    own_out[...] = hidden_units(near2[...])
+    own_out[...] = hidden_units(near2[:, :model])
+    for i in order:
+        far_hops[i].wait_recv()
+        rows_at = piece[swap[i]]
+        joined = own_out[rows_at] + far_in[piece[i], :model].astype(jnp.float32)
+        out2[rows_at, :model] = joined.astype(jnp.bfloat16)
+        last_hops[i].start()
     back_down.start()
     back_up.start()
-    far_down.wait_recv()
-    out2[first] = (own_out[first] + far_in[second].astype(jnp.float32)).astype(jnp.bfloat16)
-    last_down.start()
-    far_up.wait_recv()
-    out2[second] = (own_out[second] + far_in[first].astype(jnp.float32)).astype(jnp.bfloat16)
-    last_up.start()
     finals.finish_x()
     finals.start_z2()
     edges.finish_z()
     edges.start_x()
-    own_out[...] = hidden_units(normed_ref[...]) + middle_ref[...]
+    own_out[...] = hidden_units(normed_ref[:, :model]) + middle_ref[...]
     finals.finish_z2()
     finals.start_core2()
     edges.finish_x()
@@ -988,22 +1121,21 @@
         owned = info[12 + r] == me
         edge = jnp.where(owned, gathered[r * EDGE : (r + 1) * EDGE], edge)
     new_edge_ref[...] = edge.astype(jnp.bfloat16)
+    for i in order:
+        last_hops[i].wait_recv()
     back_down.wait_recv()
     back_up.wait_recv()
-    last_up.wait_recv()
-    last_down.wait_recv()
-    total = own_out[...] + low_in[...].astype(jnp.float32) + high_in[...].astype(jnp.float32)
+    total = own_out[...] + low_in[:, :model].astype(jnp.float32)
+    total = total + high_in[:, :model].astype(jnp.float32)
     out_ref[...] = jnp.transpose(total).astype(jnp.bfloat16)
-    for copy in (
-        up_a, down_b, up_a2, down_b2, up_b, down_a,
-        far_up, far_down, back_down, back_up, last_up, last_down,
-    ):
+    for copy in out_hops + on_hops + far_hops + last_hops + [up_b, down_a, back_down, back_up]:
         copy.wait_send()
 
 
 def mlp_call(devices, info, args, weights, rows, model, inner, requests):
     f32, bf16 = jnp.float32, jnp.bfloat16
     hidden = weights[0].shape[1]
+    wide = padded(model)
     return pl.pallas_call(
         functools.partial(mlp_stage, devices),
         out_shape=(
@@ -1014,7 +1146,7 @@
         in_specs=[sspec()] + [hspec()] * (len(args) + len(weights)),
         out_specs=tuple([vspec()] * 3),
         scratch_shapes=[
-            VMEM((rows, model), bf16),
+            VMEM((rows, wide), bf16),
             VMEM((rows, model), f32),
             VMEM((requests, STATE, inner), f32),
             VMEM((16, inner), f32),
@@ -1022,17 +1154,17 @@
             VMEM((model, hidden), bf16),
             VMEM((model, hidden), bf16),
             pltpu.SemaphoreType.DMA((7,)),
-            VMEM((rows, model), bf16),
-            VMEM((rows, model), bf16),
-            VMEM((rows, model), bf16),
-            VMEM((rows, model), bf16),
-            VMEM((rows, model), bf16),
-            VMEM((rows, model), bf16),
+            VMEM((rows, wide), bf16),
+            VMEM((rows, wide), bf16),
+            VMEM((rows, wide), bf16),
+            VMEM((rows, wide), bf16),
+            VMEM((rows, wide), bf16),
+            VMEM((rows, wide), bf16),
             VMEM((rows, model), f32),
-            VMEM((rows, model), bf16),
-            VMEM((rows, model), bf16),
-            VMEM((rows, model), bf16),
-            pltpu.SemaphoreType.DMA((2, 12)),
+            VMEM((rows, wide), bf16),
+            VMEM((rows, wide), bf16),
+            VMEM((rows, wide), bf16),
+            pltpu.SemaphoreType.DMA((2, 20)),
             VMEM((requests, 16, inner), bf16),
             VMEM((1, 16, inner), bf16),
         ]
@@ -1100,7 +1232,7 @@
             jnp.reshape(place * rows, (1,)).astype(jnp.int32),
         ]
     )
-    mixed, step, proj, enter, last_edge, start_state, params = front_call(
+    mixed, step, y, pre, proj, enter, last_edge, start_state, params = front_call(
         devices,
         info,
         (
@@ -1121,9 +1253,9 @@
         x_proj.shape[1],
         requests,
     )
-    middle, normed, finals = scan_call(
+    middle, normed, finals = join_call(
         info,
-        (mixed, step, proj, enter, start_state, params, hidden_in[0].T),
+        (y, pre, step, mixed, proj, enter, start_state, params, hidden_in[0].T),
         out_proj.T,
         rows,
         inner,

time: 107 us -> 111 us (1.037)
  Pallas kernels: 105 us -> 109 us
    pallas_call x1, Pallas kernels: 18.5 us -> 12.3 us  [join_call(): pl.pallas_call(join_stage, out_shape=(jax.ShapeDtypeStruct((rows, model),...]
    pallas_call x1, Pallas kernels: 38.4 us -> 44.5 us  [mlp_call(): pl.pallas_call(functools.partial(mlp_stage, devices), out_shape=(jax.Shap...]
    pallas_call x1, Pallas kernels: 46.3 us -> 49.9 us  [front_call(): pl.pallas_call(functools.partial(front_stage, devices), out_shape=(jax.Sh...]
where the time goes in v4:
time: 111 us
  Pallas kernels  109 us (98%)
  local copies, waits for them, and re-layouts  1.3 us (1%)
    pallas_call x1, Pallas kernels, front_call(): pl.pallas_call(functools.partial(front_stage, devices), out_shape=(jax.Sh...  49.9 us
    pallas_call x1, Pallas kernels, mlp_call(): pl.pallas_call(functools.partial(mlp_stage, devices), out_shape=(jax.Shap...  44.5 us
    pallas_call x1, Pallas kernels, join_call(): pl.pallas_call(join_stage, out_shape=(jax.ShapeDtypeStruct((rows, model),...  12.3 us

profile of v4, /device:TPU:0, one launch (start us, length us, event | category | flops | bytes accessed | tf_op | source)
XLA Modules:
  0.0 110.6 jit_solution(11474558082300748260)
XLA Ops:
  0.6 1.3 %concatenate.3.info = s32[17]{0:T(128)} concatenate(s32[4]{0:T(128)} %bitcast.21, s32[4]{0:T(128)} %bitcast.22, s32[4]{0:T(128)} %bitcast.23, s32[4]{0:T(128)} %bitcast.24, s32[1]{0:T(128)} %bitcast.4), dimensions={0} | concatenate | bytes 136 | tf_op jit(solution)/shard_map/concatenate | solution.py:1226
  1.9 49.9 %front_stage.1 = (f32[128,3200]{1,0:T(8,128)}, f32[128,3200]{1,0:T(8,128)}, f32[128,3200]{1,0:T(8,128)}, f32[128,3200]{1,0:T(8,128)}, f32[128,132]{1,0:T(8,128)}...) custom-call(s32[17]{0:T(128)} %concatenate.3.info, ...), custom_call_target="tpu_custom_call" | custom-call | flops 400000000 | bytes 8000000 | tf_op jit(solution)/shard_map/front_stage/pallas_call | solution.py:676
  51.8 12.3 %join_stage.1 = (f32[128,1600]{1,0:T(8,128)}, bf16[128,1664]{1,0:T(8,128)(2,1)}, f32[4,16,3200]{2,1,0:T(8,128)}) custom-call(s32[17]{0:T(128)} %concatenate.3.info, f32[128,3200]{1,0:T(8,128)} %get-tuple-element.21.y_hbm, f32[128,3200]{1,0:T(8,128)} %get-tuple-element.22.pre_hbm, f32[128,3200]{1,0:T(8,128)} %get-tuple-element.23.step_hbm, ...), custom_call_target="tpu_custom_call" | custom-call | flops 1400000000 | bytes 18000000 | tf_op jit(solution)/shard_map/join_stage/pallas_call | solution.py:922
  64.2 44.5 %mlp_stage.1 = (bf16[1600,128]{1,0:T(8,128)(2,1)}, f32[16,3200]{1,0:T(8,128)}, bf16[3,3200]{1,0:T(4,128)(2,1)}) custom-call(s32[17]{0:T(128)} %concatenate.3.info, bf16[128,1664]{1,0:T(8,128)(2,1)} %get-tuple-element.29.normed_hbm, f32[128,1600]{1,0:T(8,128)} %get-tuple-element.30.middle_hbm, f32[4,16,3200]{2,1,0:T(8,128)} %get-tuple-element.31.final_hbm, ...), custom_call_target="tpu_custom_call" | custom-call | flops 7000000000 | bytes 16000000 | tf_op jit(solution)/shard_map/mlp_stage/pallas_call | solution.py:1139
  108.7 1.9 %handing_stage.1 = (bf16[1600,128]{1,0:T(8,128)(2,1)}, f32[16,3200]{1,0:T(8,128)}, bf16[3,3200]{1,0:T(4,128)(2,1)}) custom-call(bf16[1600,128]{1,0:T(8,128)(2,1)} %get-tuple-element.33.refs_0_, f32[16,3200]{1,0:T(8,128)} %get-tuple-element.34.refs_1_, bf16[3,3200]{1,0:T(4,128)(2,1)} %get-tuple-element.35.refs_2_), custom_call_target="tpu_custom_call" | custom-call | tf_op jit(solution)/shard_map/handing_stage/pallas_call | solution.py:1190

commit v5 on v3

--- a/solution.py
+++ b/solution.py
@@ -39,6 +39,10 @@
 def layout_of(devices):
     depth = 4 if devices >= 32 else 2
     return devices // (2 * depth), depth
+
+
+def padded(width):
+    return -(-width // LANES) * LANES
 
 
 def half_width(inner):
@@ -327,14 +331,10 @@
     edge_sum.finish_z()
     edge_sum.start_x()
     state_sum.start_z()
-    edge_sum.finish_x()
-    edge_sum.start_core2()
-    edge_sum.finish_core2(edge3_ref)
-    edge_ref = edge3_ref.at[0]
     halo_copy.wait()
+    ext[pl.ds(0, 16), :] = halo_ref[...].astype(jnp.float32)
     width = col_block(inner)
     rank = dt_proj_ref.shape[0]
-    ext[pl.ds(0, 16), :] = halo_ref[...].astype(jnp.float32)
     first_pos = info[16]
     position = first_pos + lax.broadcasted_iota(jnp.int32, (rows, LANES), 0)
     marks = [segment(info, r, rows) for r in range(requests)]
@@ -362,13 +362,29 @@
         keep[lag] = jnp.concatenate([offset] * (width // LANES), axis=1) >= lag
     for first in range(0, inner, width):
         cols = pl.ds(first, width)
-        edges = edge_ref[:, cols]
         total = conv_b_ref[:, cols] + conv_w_ref[pl.ds(3, 1), cols] * ext[pl.ds(16, rows), cols]
         for lag in (1, 2, 3):
             near = ext[pl.ds(16 - lag, rows), cols]
-            far = jnp.dot(hots[lag - 1], edges, preferred_element_type=jnp.float32)
-            row = jnp.where(keep[lag], near, far)
+            row = jnp.where(keep[lag], near, 0.0)
             total = total + conv_w_ref[pl.ds(3 - lag, 1), cols] * row
+        suffix[:, cols] = total
+    edge_sum.finish_x()
+    edge_sum.start_core2()
+    edge_sum.finish_core2(edge3_ref)
+    edge_ref = edge3_ref.at[0]
+    hot = jnp.concatenate(hots * 3, axis=1)
+    for first in range(0, inner, width):
+        cols = pl.ds(first, width)
+        edges = edge_ref[:, cols].astype(jnp.float32)
+        far = jnp.concatenate(
+            [conv_w_ref[pl.ds(3 - lag, 1), cols] * edges for lag in (1, 2, 3)], axis=0
+        )
+        high = far.astype(jnp.bfloat16)
+        rest = far - high.astype(jnp.float32)
+        mid = rest.astype(jnp.bfloat16)
+        low = (rest - mid.astype(jnp.float32)).astype(jnp.bfloat16)
+        far = jnp.concatenate([high, mid, low], axis=0)
+        total = suffix[:, cols] + jnp.dot(hot, far, preferred_element_type=jnp.float32)
         mixed = (total / (1.0 + jnp.exp(-total))).astype(jnp.bfloat16)
         mixed_b[:, cols] = mixed
         mixed_ref[:, cols] = mixed.astype(jnp.float32)
@@ -635,6 +651,22 @@
     )(info, *args)
 
 
+def row_sums(parts):
+    row = lax.broadcasted_iota(jnp.int32, parts[0].shape, 0)
+    for step in (4, 2, 1):
+        odd = (row // step) % 2 == 1
+        joined = []
+        for i in range(step):
+            a, b = parts[i], parts[i + step]
+            keep, move = jnp.where(odd, b, a), jnp.where(odd, a, b)
+            moved = pltpu.roll(move, step, 0)
+            if step < 4:
+                moved = jnp.where(odd, moved, pltpu.roll(move, 8 - step, 0))
+            joined.append(keep + moved)
+        parts = joined
+    return parts[0]
+
+
 def scan_stage(
     info,
     mixed_hbm,
@@ -706,7 +738,7 @@
             low = d_low * state[2 * j] + b_low * p_row
             high = d_high * state[2 * j + 1] + b_high * p_row
             new += [low, high]
-            outs.append(jnp.sum(c_low * low + c_high * high, axis=0, keepdims=True))
+            outs.append(c_low * low + c_high * high)
         return outs, tuple(new)
 
     def one_block(g, carry):
@@ -736,7 +768,7 @@
                 for j in range(tiles):
                     kept[j].append(outs[j])
             for j in range(tiles):
-                y = jnp.concatenate(kept[j], axis=0)
+                y = row_sums(kept[j])
                 if limits is not None:
                     at = row + lax.broadcasted_iota(jnp.int32, (8, LANES), 0)
                     y = jnp.where(
@@ -790,7 +822,10 @@
         )
     middle_ref[...] = middle
     scale = lax.rsqrt(jnp.mean(middle * middle, axis=1, keepdims=True) + NORM_EPS)
-    normed_ref[...] = (middle * scale * param_ref[8:9, :model]).astype(jnp.bfloat16)
+    normed = (middle * scale * param_ref[8:9, :model]).astype(jnp.bfloat16)
+    if normed_ref.shape[1] > model:
+        normed_ref[...] = jnp.zeros_like(normed_ref)
+    normed_ref[:, :model] = normed
     keep_final.wait()
 
 
@@ -800,7 +835,7 @@
         scan_stage,
         out_shape=(
             jax.ShapeDtypeStruct((rows, model), f32),
-            jax.ShapeDtypeStruct((rows, model), jnp.bfloat16),
+            jax.ShapeDtypeStruct((rows, padded(model)), jnp.bfloat16),
             jax.ShapeDtypeStruct((requests, STATE, inner), f32),
         ),
         in_specs=[sspec()] + [hspec()] * 2 + [vspec()] * (len(args) - 3) + [hspec()] * 2,
@@ -863,7 +898,7 @@
     full_edge,
     *spread_refs,
 ):
-    rows, model = normed_ref.shape
+    rows, model = middle_ref.shape
     half = rows // 2
     inner = final_ref.shape[2]
     requests = final_ref.shape[0]
@@ -901,22 +936,30 @@
             device_id_type=MESH_ID,
         )
 
+    piece = [pl.ds(i * (half // 2), half // 2) for i in range(4)]
     first, second = pl.ds(0, half), pl.ds(half, half)
-    up_a = hop(normed_ref.at[first], near1.at[first], 0, above)
-    down_b = hop(normed_ref.at[second], near1.at[second], 1, below)
-    up_a2 = hop(near1.at[first], far.at[first], 2, above)
-    down_b2 = hop(near1.at[second], far.at[second], 3, below)
-    up_b = hop(normed_ref.at[second], near2.at[first], 4, above)
-    down_a = hop(normed_ref.at[first], near2.at[second], 5, below)
-    far_up = hop(far_out.at[first], far_in.at[first], 6, above)
-    far_down = hop(far_out.at[second], far_in.at[second], 7, below)
-    back_down = hop(out1.at[first], high_in.at[first], 8, below)
-    back_up = hop(out1.at[second], low_in.at[second], 9, above)
-    last_down = hop(out2.at[first], high_in.at[second], 10, below)
-    last_up = hop(out2.at[second], low_in.at[first], 11, above)
+    toward = [above, above, below, below]
+    out_hops = [hop(normed_ref.at[piece[i]], near1.at[piece[i]], i, toward[i]) for i in range(4)]
+    on_hops = [hop(near1.at[piece[i]], far.at[piece[i]], 4 + i, toward[i]) for i in range(4)]
+    up_b = hop(normed_ref.at[second], near2.at[first], 8, above)
+    down_a = hop(normed_ref.at[first], near2.at[second], 9, below)
+    far_hops = [hop(far_out.at[piece[i]], far_in.at[piece[i]], 10 + i, toward[i]) for i in range(4)]
+    back_down = hop(out1.at[first], high_in.at[first], 14, below)
+    back_up = hop(out1.at[second], low_in.at[second], 15, above)
+    swap = [2, 3, 0, 1]
+    last_hops = [
+        hop(
+            out2.at[piece[swap[i]]],
+            (low_in if i < 2 else high_in).at[piece[i]],
+            16 + i,
+            toward[i],
+        )
+        for i in range(4)
+    ]
+    order = (0, 2, 1, 3)
     fetches[0].wait()
-    up_a.start()
-    down_b.start()
+    for i in order:
+        out_hops[i].start()
     per = len(Spread.scratch(devices, inner, 1, False))
     finals = Spread(devices, inner, requests, True, spread_refs[:per])
     edges = Spread(devices, inner, 1, False, spread_refs[per:])
@@ -939,39 +982,38 @@
     finals.finish_core()
     finals.start_z()
     edges.finish_core()
-    up_a.wait_recv()
-    up_a2.start()
-    down_b.wait_recv()
-    down_b2.start()
+    for i in order:
+        out_hops[i].wait_recv()
+        on_hops[i].start()
+    up_b.start()
+    down_a.start()
     for copy in fetches[3:]:
         copy.wait()
-    out1[...] = hidden_units(near1[...]).astype(jnp.bfloat16)
-    up_b.start()
-    down_a.start()
-    up_a2.wait_recv()
-    down_b2.wait_recv()
-    far_out[...] = hidden_units(far[...]).astype(jnp.bfloat16)
-    far_up.start()
-    far_down.start()
+    out1[:, :model] = hidden_units(near1[:, :model]).astype(jnp.bfloat16)
+    for i in order:
+        on_hops[i].wait_recv()
+    far_out[:, :model] = hidden_units(far[:, :model]).astype(jnp.bfloat16)
+    for i in order:
+        far_hops[i].start()
     finals.finish_z()
     finals.start_x()
     edges.start_z()
     up_b.wait_recv()
     down_a.wait_recv()
-    own_out[...] = hidden_units(near2[...])
+    own_out[...] = hidden_units(near2[:, :model])
+    for i in order:
+        far_hops[i].wait_recv()
+        rows_at = piece[swap[i]]
+        joined = own_out[rows_at] + far_in[piece[i], :model].astype(jnp.float32)
+        out2[rows_at, :model] = joined.astype(jnp.bfloat16)
+        last_hops[i].start()
     back_down.start()
     back_up.start()
-    far_down.wait_recv()
-    out2[first] = (own_out[first] + far_in[second].astype(jnp.float32)).astype(jnp.bfloat16)
-    last_down.start()
-    far_up.wait_recv()
-    out2[second] = (own_out[second] + far_in[first].astype(jnp.float32)).astype(jnp.bfloat16)
-    last_up.start()
     finals.finish_x()
     finals.start_z2()
     edges.finish_z()
     edges.start_x()
-    own_out[...] = hidden_units(normed_ref[...]) + middle_ref[...]
+    own_out[...] = hidden_units(normed_ref[:, :model]) + middle_ref[...]
     finals.finish_z2()
     finals.start_core2()
     edges.finish_x()
@@ -988,22 +1030,21 @@
         owned = info[12 + r] == me
         edge = jnp.where(owned, gathered[r * EDGE : (r + 1) * EDGE], edge)
     new_edge_ref[...] = edge.astype(jnp.bfloat16)
+    for i in order:
+        last_hops[i].wait_recv()
     back_down.wait_recv()
     back_up.wait_recv()
-    last_up.wait_recv()
-    last_down.wait_recv()
-    total = own_out[...] + low_in[...].astype(jnp.float32) + high_in[...].astype(jnp.float32)
+    total = own_out[...] + low_in[:, :model].astype(jnp.float32)
+    total = total + high_in[:, :model].astype(jnp.float32)
     out_ref[...] = jnp.transpose(total).astype(jnp.bfloat16)
-    for copy in (
-        up_a, down_b, up_a2, down_b2, up_b, down_a,
-        far_up, far_down, back_down, back_up, last_up, last_down,
-    ):
+    for copy in out_hops + on_hops + far_hops + last_hops + [up_b, down_a, back_down, back_up]:
         copy.wait_send()
 
 
 def mlp_call(devices, info, args, weights, rows, model, inner, requests):
     f32, bf16 = jnp.float32, jnp.bfloat16
     hidden = weights[0].shape[1]
+    wide = padded(model)
     return pl.pallas_call(
         functools.partial(mlp_stage, devices),
         out_shape=(
@@ -1014,7 +1055,7 @@
         in_specs=[sspec()] + [hspec()] * (len(args) + len(weights)),
         out_specs=tuple([vspec()] * 3),
         scratch_shapes=[
-            VMEM((rows, model), bf16),
+            VMEM((rows, wide), bf16),
             VMEM((rows, model), f32),
             VMEM((requests, STATE, inner), f32),
             VMEM((16, inner), f32),
@@ -1022,17 +1063,17 @@
             VMEM((model, hidden), bf16),
             VMEM((model, hidden), bf16),
             pltpu.SemaphoreType.DMA((7,)),
-            VMEM((rows, model), bf16),
-            VMEM((rows, model), bf16),
-            VMEM((rows, model), bf16),
-            VMEM((rows, model), bf16),
-            VMEM((rows, model), bf16),
-            VMEM((rows, model), bf16),
+            VMEM((rows, wide), bf16),
+            VMEM((rows, wide), bf16),
+            VMEM((rows, wide), bf16),
+            VMEM((rows, wide), bf16),
+            VMEM((rows, wide), bf16),
+            VMEM((rows, wide), bf16),
             VMEM((rows, model), f32),
-            VMEM((rows, model), bf16),
-            VMEM((rows, model), bf16),
-            VMEM((rows, model), bf16),
-            pltpu.SemaphoreType.DMA((2, 12)),
+            VMEM((rows, wide), bf16),
+            VMEM((rows, wide), bf16),
+            VMEM((rows, wide), bf16),
+            pltpu.SemaphoreType.DMA((2, 20)),
             VMEM((requests, 16, inner), bf16),
             VMEM((1, 16, inner), bf16),
         ]

time: 107 us -> 104 us (0.972)
  Pallas kernels: 105 us -> 102 us
    pallas_call x1, Pallas kernels: 38.4 us -> 37 us  [mlp_call(): pl.pallas_call(functools.partial(mlp_stage, devices), out_shape=(jax.Shap...]
where the time goes in v5:
time: 104 us
  Pallas kernels  102 us (98%)
  local copies, waits for them, and re-layouts  1.3 us (1%)
    pallas_call x1, Pallas kernels, front_call(): pl.pallas_call(functools.partial(front_stage, devices), out_shape=(jax.Sh...  45.4 us
    pallas_call x1, Pallas kernels, mlp_call(): pl.pallas_call(functools.partial(mlp_stage, devices), out_shape=(jax.Shap...  37 us
    pallas_call x1, Pallas kernels, scan_call(): pl.pallas_call(scan_stage, out_shape=(jax.ShapeDtypeStruct((rows, model),...  17.8 us

profile of v5, /device:TPU:0, one launch (start us, length us, event | category | flops | bytes accessed | tf_op | source)
XLA Modules:
  0.0 104.1 jit_solution(814885688449757122)
XLA Ops:
  0.6 1.3 %concatenate.3.info = s32[17]{0:T(128)} concatenate(s32[4]{0:T(128)} %bitcast.21, s32[4]{0:T(128)} %bitcast.22, s32[4]{0:T(128)} %bitcast.23, s32[4]{0:T(128)} %bitcast.24, s32[1]{0:T(128)} %bitcast.4), dimensions={0} | concatenate | bytes 136 | tf_op jit(solution)/shard_map/concatenate | solution.py:1135
  1.9 45.4 %front_stage.1 = (f32[128,3200]{1,0:T(8,128)}, f32[128,3200]{1,0:T(8,128)}, f32[128,132]{1,0:T(8,128)}, f32[16,3200]{1,0:T(8,128)}, f32[16,3200]{1,0:T(8,128)}, ...) custom-call(s32[17]{0:T(128)} %concatenate.3.info, f32[4,3200]{1,0:T(4,128)} %taps_ref.1, f32[3200]{0:T(1024)} %conv_b_flat.1, ...), custom_call_target="tpu_custom_call" | custom-call | flops 400000000 | bytes 8000000 | tf_op jit(solution)/shard_map/front_stage/pallas_call | solution.py:597
  47.3 17.8 %scan_stage.1 = (f32[128,1600]{1,0:T(8,128)}, bf16[128,1664]{1,0:T(8,128)(2,1)}, f32[4,16,3200]{2,1,0:T(8,128)}) custom-call(s32[17]{0:T(128)} %concatenate.3.info, f32[128,3200]{1,0:T(8,128)} %get-tuple-element.19.mixed_hbm, f32[128,3200]{1,0:T(8,128)} %get-tuple-element.20.step_hbm, f32[128,132]{1,0:T(8,128)} %get-tuple-element.21.proj_ref, ...), custom_call_target="tpu_custom_call" | custom-call | flops 1400000000 | bytes 18000000 | tf_op jit(solution)/shard_map/scan_stage/pallas_call | solution.py:834
  65.2 37.0 %mlp_stage.1 = (bf16[1600,128]{1,0:T(8,128)(2,1)}, f32[16,3200]{1,0:T(8,128)}, bf16[3,3200]{1,0:T(4,128)(2,1)}) custom-call(s32[17]{0:T(128)} %concatenate.3.info, bf16[128,1664]{1,0:T(8,128)(2,1)} %get-tuple-element.25.normed_hbm, f32[128,1600]{1,0:T(8,128)} %get-tuple-element.26.middle_hbm, f32[4,16,3200]{2,1,0:T(8,128)} %get-tuple-element.27.final_hbm, ...), custom_call_target="tpu_custom_call" | custom-call | flops 7000000000 | bytes 16000000 | tf_op jit(solution)/shard_map/mlp_stage/pallas_call | solution.py:1048
  102.1 1.9 %handing_stage.1 = (bf16[1600,128]{1,0:T(8,128)(2,1)}, f32[16,3200]{1,0:T(8,128)}, bf16[3,3200]{1,0:T(4,128)(2,1)}) custom-call(bf16[1600,128]{1,0:T(8,128)(2,1)} %get-tuple-element.29.refs_0_, f32[16,3200]{1,0:T(8,128)} %get-tuple-element.30.refs_1_, bf16[3,3200]{1,0:T(4,128)(2,1)} %get-tuple-element.31.refs_2_), custom_call_target="tpu_custom_call" | custom-call | tf_op jit(solution)/shard_map/handing_stage/pallas_call | solution.py:1099

commit v6 on v5

--- a/solution.py
+++ b/solution.py
@@ -370,6 +370,8 @@
         suffix[:, cols] = total
     edge_sum.finish_x()
     edge_sum.start_core2()
+    state_sum.finish_z()
+    state_sum.start_x()
     edge_sum.finish_core2(edge3_ref)
     edge_ref = edge3_ref.at[0]
     hot = jnp.concatenate(hots * 3, axis=1)
@@ -389,8 +391,6 @@
         mixed_b[:, cols] = mixed
         mixed_ref[:, cols] = mixed.astype(jnp.float32)
 
-    state_sum.finish_z()
-    state_sum.start_x()
     keep_mixed = pltpu.make_async_copy(mixed_ref, mixed_hbm, keep_sems.at[0])
     keep_mixed.start()
     proj = lax.dot_general(
@@ -1007,8 +1007,9 @@
         joined = own_out[rows_at] + far_in[piece[i], :model].astype(jnp.float32)
         out2[rows_at, :model] = joined.astype(jnp.bfloat16)
         last_hops[i].start()
-    back_down.start()
-    back_up.start()
+        if i == 2:
+            back_down.start()
+            back_up.start()
     finals.finish_x()
     finals.start_z2()
     edges.finish_z()

time: 104 us -> 103 us (level)
    pallas_call x1, Pallas kernels: 45.4 us -> 43.7 us  [front_call(): pl.pallas_call(functools.partial(front_stage, devices), out_shape=(jax.Sh...]
where the time goes in v6:
time: 103 us
  Pallas kernels  101 us (98%)
  local copies, waits for them, and re-layouts  1.3 us (1%)
    pallas_call x1, Pallas kernels, front_call(): pl.pallas_call(functools.partial(front_stage, devices), out_shape=(jax.Sh...  43.7 us
    pallas_call x1, Pallas kernels, mlp_call(): pl.pallas_call(functools.partial(mlp_stage, devices), out_shape=(jax.Shap...  37.1 us
    pallas_call x1, Pallas kernels, scan_call(): pl.pallas_call(scan_stage, out_shape=(jax.ShapeDtypeStruct((rows, model),...  17.8 us

profile of v6, /device:TPU:0, one launch (start us, length us, event | category | flops | bytes accessed | tf_op | source)
XLA Modules:
  0.0 102.5 jit_solution(881989644623822210)
XLA Ops:
  0.6 1.3 %concatenate.3.info = s32[17]{0:T(128)} concatenate(s32[4]{0:T(128)} %bitcast.21, s32[4]{0:T(128)} %bitcast.22, s32[4]{0:T(128)} %bitcast.23, s32[4]{0:T(128)} %bitcast.24, s32[1]{0:T(128)} %bitcast.4), dimensions={0} | concatenate | bytes 136 | tf_op jit(solution)/shard_map/concatenate | solution.py:1136
  1.9 43.7 %front_stage.1 = (f32[128,3200]{1,0:T(8,128)}, f32[128,3200]{1,0:T(8,128)}, f32[128,132]{1,0:T(8,128)}, f32[16,3200]{1,0:T(8,128)}, f32[16,3200]{1,0:T(8,128)}, ...) custom-call(s32[17]{0:T(128)} %concatenate.3.info, f32[4,3200]{1,0:T(4,128)} %taps_ref.1, f32[3200]{0:T(1024)} %conv_b_flat.1, ...), custom_call_target="tpu_custom_call" | custom-call | flops 400000000 | bytes 8000000 | tf_op jit(solution)/shard_map/front_stage/pallas_call | solution.py:597
  45.6 17.8 %scan_stage.1 = (f32[128,1600]{1,0:T(8,128)}, bf16[128,1664]{1,0:T(8,128)(2,1)}, f32[4,16,3200]{2,1,0:T(8,128)}) custom-call(s32[17]{0:T(128)} %concatenate.3.info, f32[128,3200]{1,0:T(8,128)} %get-tuple-element.19.mixed_hbm, f32[128,3200]{1,0:T(8,128)} %get-tuple-element.20.step_hbm, f32[128,132]{1,0:T(8,128)} %get-tuple-element.21.proj_ref, ...), custom_call_target="tpu_custom_call" | custom-call | flops 1400000000 | bytes 18000000 | tf_op jit(solution)/shard_map/scan_stage/pallas_call | solution.py:834
  63.4 37.1 %mlp_stage.1 = (bf16[1600,128]{1,0:T(8,128)(2,1)}, f32[16,3200]{1,0:T(8,128)}, bf16[3,3200]{1,0:T(4,128)(2,1)}) custom-call(s32[17]{0:T(128)} %concatenate.3.info, bf16[128,1664]{1,0:T(8,128)(2,1)} %get-tuple-element.25.normed_hbm, f32[128,1600]{1,0:T(8,128)} %get-tuple-element.26.middle_hbm, f32[4,16,3200]{2,1,0:T(8,128)} %get-tuple-element.27.final_hbm, ...), custom_call_target="tpu_custom_call" | custom-call | flops 7000000000 | bytes 16000000 | tf_op jit(solution)/shard_map/mlp_stage/pallas_call | solution.py:1049
  100.6 1.9 %handing_stage.1 = (bf16[1600,128]{1,0:T(8,128)(2,1)}, f32[16,3200]{1,0:T(8,128)}, bf16[3,3200]{1,0:T(4,128)(2,1)}) custom-call(bf16[1600,128]{1,0:T(8,128)(2,1)} %get-tuple-element.29.refs_0_, f32[16,3200]{1,0:T(8,128)} %get-tuple-element.30.refs_1_, bf16[3,3200]{1,0:T(4,128)(2,1)} %get-tuple-element.31.refs_2_), custom_call_target="tpu_custom_call" | custom-call | tf_op jit(solution)/shard_map/handing_stage/pallas_call | solution.py:1100

commit v7 on v6

--- a/solution.py
+++ b/solution.py
@@ -672,8 +672,8 @@
     mixed_hbm,
     step_hbm,
     proj_ref,
-    enter_ref,
-    start_ref,
+    enter_hbm,
+    start_hbm,
     param_ref,
     hidden_hbm,
     out_w_hbm,
@@ -683,6 +683,9 @@
     mixed_ref,
     step_ref,
     final_ref,
+    enter_ref,
+    start_ref,
+    seed_sems,
     block_sems,
     final_sem,
     bc_wide,
@@ -697,6 +700,12 @@
     width = col_block(inner)
     tiles = width // LANES
     rank = proj_ref.shape[1] - 2 * STATE
+    seeds = (
+        pltpu.make_async_copy(enter_hbm, enter_ref, seed_sems.at[0]),
+        pltpu.make_async_copy(start_hbm, start_ref, seed_sems.at[1]),
+    )
+    for copy in seeds:
+        copy.start()
     width = col_block(step_ref.shape[1])
 
     def block_copies(g):
@@ -807,6 +816,8 @@
         ssm_b[:, pl.ds(base, width)] = y.astype(jnp.bfloat16)
         return carry
 
+    for copy in seeds:
+        copy.wait()
     lax.fori_loop(0, inner // width, one_block, 0)
     keep_final = pltpu.make_async_copy(final_ref, final_hbm, final_sem)
     keep_final.start()
@@ -838,12 +849,20 @@
             jax.ShapeDtypeStruct((rows, padded(model)), jnp.bfloat16),
             jax.ShapeDtypeStruct((requests, STATE, inner), f32),
         ),
-        in_specs=[sspec()] + [hspec()] * 2 + [vspec()] * (len(args) - 3) + [hspec()] * 2,
+        in_specs=[sspec()]
+        + [hspec()] * 2
+        + [vspec()]
+        + [hspec()] * 2
+        + [vspec()] * (len(args) - 6)
+        + [hspec()] * 2,
         out_specs=tuple([vspec()] * 2 + [hspec()]),
         scratch_shapes=[
             VMEM((rows, inner), f32),
             VMEM((rows, inner), f32),
             VMEM((requests, STATE, inner), f32),
+            VMEM((STATE, inner), f32),
+            VMEM((requests, STATE, inner), jnp.bfloat16),
+            pltpu.SemaphoreType.DMA((2,)),
             pltpu.SemaphoreType.DMA((2, inner // col_block(inner))),
             pltpu.SemaphoreType.DMA,
             VMEM((rows, 2 * STATE, LANES), f32),

time: 103 us -> 104 us (level)
  no operation moved by 1% of the time
where the time goes in v7:
time: 104 us; the launch traced here: 103 us
  Pallas kernels  101 us (97%)
  local copies, waits for them, and re-layouts  1.3 us (1%)
    pallas_call x1, Pallas kernels, front_call(): pl.pallas_call(functools.partial(front_stage, devices), out_shape=(jax.Sh...  43.7 us
    pallas_call x1, Pallas kernels, mlp_call(): pl.pallas_call(functools.partial(mlp_stage, devices), out_shape=(jax.Shap...  37.1 us
    pallas_call x1, Pallas kernels, scan_call(): pl.pallas_call(scan_stage, out_shape=(jax.ShapeDtypeStruct((rows, model),...  18.3 us

profile of v7, /device:TPU:0, one launch (start us, length us, event | category | flops | bytes accessed | tf_op | source)
XLA Modules:
  0.0 103.0 jit_solution(1225803306760773470)
XLA Ops:
  0.6 1.3 %concatenate.3.info = s32[17]{0:T(128)} concatenate(s32[4]{0:T(128)} %bitcast.21, s32[4]{0:T(128)} %bitcast.22, s32[4]{0:T(128)} %bitcast.23, s32[4]{0:T(128)} %bitcast.24, s32[1]{0:T(128)} %bitcast.4), dimensions={0} | concatenate | bytes 136 | tf_op jit(solution)/shard_map/concatenate | solution.py:1155
  1.9 43.7 %front_stage.1 = (f32[128,3200]{1,0:T(8,128)}, f32[128,3200]{1,0:T(8,128)}, f32[128,132]{1,0:T(8,128)}, f32[16,3200]{1,0:T(8,128)}, f32[16,3200]{1,0:T(8,128)}, ...) custom-call(s32[17]{0:T(128)} %concatenate.3.info, f32[4,3200]{1,0:T(4,128)} %taps_ref.1, f32[3200]{0:T(1024)} %conv_b_flat.1, ...), custom_call_target="tpu_custom_call" | custom-call | flops 400000000 | bytes 8000000 | tf_op jit(solution)/shard_map/front_stage/pallas_call | solution.py:597
  45.6 18.3 %scan_stage.1 = (f32[128,1600]{1,0:T(8,128)}, bf16[128,1664]{1,0:T(8,128)(2,1)}, f32[4,16,3200]{2,1,0:T(8,128)}) custom-call(s32[17]{0:T(128)} %concatenate.3.info, f32[128,3200]{1,0:T(8,128)} %get-tuple-element.19.mixed_hbm, f32[128,3200]{1,0:T(8,128)} %get-tuple-element.20.step_hbm, f32[128,132]{1,0:T(8,128)} %get-tuple-element.21.proj_ref, ...), custom_call_target="tpu_custom_call" | custom-call | flops 1400000000 | bytes 18000000 | tf_op jit(solution)/shard_map/scan_stage/pallas_call | solution.py:845
  64.0 37.1 %mlp_stage.1 = (bf16[1600,128]{1,0:T(8,128)(2,1)}, f32[16,3200]{1,0:T(8,128)}, bf16[3,3200]{1,0:T(4,128)(2,1)}) custom-call(s32[17]{0:T(128)} %concatenate.3.info, bf16[128,1664]{1,0:T(8,128)(2,1)} %get-tuple-element.25.normed_hbm, f32[128,1600]{1,0:T(8,128)} %get-tuple-element.26.middle_hbm, f32[4,16,3200]{2,1,0:T(8,128)} %get-tuple-element.27.final_hbm, ...), custom_call_target="tpu_custom_call" | custom-call | flops 7000000000 | bytes 16000000 | tf_op jit(solution)/shard_map/mlp_stage/pallas_call | solution.py:1068
  101.1 1.9 %handing_stage.1 = (bf16[1600,128]{1,0:T(8,128)(2,1)}, f32[16,3200]{1,0:T(8,128)}, bf16[3,3200]{1,0:T(4,128)(2,1)}) custom-call(bf16[1600,128]{1,0:T(8,128)(2,1)} %get-tuple-element.29.refs_0_, f32[16,3200]{1,0:T(8,128)} %get-tuple-element.30.refs_1_, bf16[3,3200]{1,0:T(4,128)(2,1)} %get-tuple-element.31.refs_2_), custom_call_target="tpu_custom_call" | custom-call | tf_op jit(solution)/shard_map/handing_stage/pallas_call | solution.py:1119
